TPU v7x, 256 devices: a whole 4x4x8 slice. The times are simulated.
256 devices in a mesh: dp: 16 (over x, y), shard: 16 (over z, core).
Axes of the slice: x: 4, y: 4, z: 8, core: 2. Of those that a mesh axis runs over, the one named last changes fastest.
Arguments:
- gradient: bfloat16 [16, 4096, 6144], P('dp', None, 'shard'), may hold values from -400 to 400
- error_buffer: bfloat16 [16, 4096, 6144], P('dp', None, 'shard'), may hold values from -6 to 6
- right_init: float32 [6144, 32], P('shard'), may hold values from -6 to 6
- first_moment: float32 [4096, 6144], P(('dp', 'shard')), may hold values from -0.06 to 0.06
- second_moment: float32 [4096, 6144], P(('dp', 'shard')), may hold values from 0.001 to 0.01
Outputs:
- error_out: bfloat16 [16, 4096, 6144], P('dp', None, 'shard')
- first_out: float32 [4096, 6144], P(('dp', 'shard'))
- second_out: float32 [4096, 6144], P(('dp', 'shard'))
- direction: float32 [4096, 6144], P(('dp', 'shard'))
All inputs are finite; a program needn't handle non-finite values.
Results may differ from a plain program's by a relative error of at most 0.009.
Values sent between devices are 32-bit elements; how exact they have to be, the bound alone decides.
A program may use at most 64 MiB of HBM per device.

v0:
```python
import jax
import jax.numpy as jnp
from jax import lax
from jax.sharding import PartitionSpec as P

D = 4096
F = 6144
R = 32


CLIP_LEVEL = 0.9
BETA_ONE = 0.9
BETA_TWO = 0.95
EPSILON = 1e-08


def cut_along(x, dim, count):
    shape = x.shape
    tiles = x.reshape(*shape[:dim], count, shape[dim] // count, *shape[dim + 1 :])
    return jnp.moveaxis(tiles, dim, 0)


def sent_and_summed(x, axis, dim):
    tiles = cut_along(x, dim, lax.axis_size(axis))
    arrived = lax.all_to_all(tiles, axis, split_axis=0, concat_axis=0, tiled=True)
    return arrived.sum(axis=0)


def sent_to_all(x, axis):
    count = lax.axis_size(axis)
    return lax.all_to_all(jnp.broadcast_to(x[None], (count, *x.shape)), axis, 0, 0, tiled=True)


def taken_together(x, axis):
    return sent_to_all(x, axis).sum(axis=0)


def laid_out(tiles, dim):
    shape = list(tiles.shape[1:])
    shape[dim] *= tiles.shape[0]
    return jnp.moveaxis(tiles, 0, dim).reshape(shape)


def collect(x, axis, dim):
    return laid_out(sent_to_all(x, axis), dim)


def orthonormal(left_raw, gram_matrix):
    width = gram_matrix.shape[0]
    ridge_shift = 1e-06 * jnp.trace(gram_matrix) / width
    lower_factor = jnp.linalg.cholesky(
        gram_matrix + ridge_shift * jnp.eye(width, dtype=jnp.float32)
    )
    return lax.linalg.triangular_solve(
        lower_factor, left_raw, left_side=False, lower=True, transpose_a=True
    )


def local(gradient, error_buffer, right_init, first_moment, second_moment):
    replica_count = lax.axis_size("dp")
    shard_count = lax.axis_size("shard")
    merged = (gradient[0].astype(jnp.float32) + error_buffer[0].astype(jnp.float32)).astype(
        jnp.bfloat16
    )
    total_rows = merged.shape[0]
    left_part = jnp.dot(merged, right_init.astype(jnp.bfloat16), preferred_element_type=jnp.float32)
    row_share = sent_and_summed(left_part, "shard", 0)
    row_share = taken_together(row_share, "dp") / replica_count
    left_raw = lax.all_gather(row_share, "shard", axis=0, tiled=True)
    gram_matrix = jnp.dot(left_raw.T, left_raw, precision=lax.Precision.HIGHEST)
    left_orth = orthonormal(left_raw, gram_matrix)
    right_part = lax.dot_general(
        merged,
        left_orth.astype(jnp.bfloat16),
        (((0,), (0,)), ((), ())),
        preferred_element_type=jnp.float32,
    )
    right_mean = taken_together(right_part, "dp") / replica_count
    update = jnp.dot(left_orth, right_mean.T, precision=lax.Precision.HIGHEST)
    error_out = (merged.astype(jnp.float32) - update).astype(jnp.bfloat16)[None]
    slab_size = total_rows // replica_count
    own_count = slab_size // shard_count
    right_full = collect(right_mean, "shard", 0)
    first_row = (lax.axis_index("dp") * shard_count + lax.axis_index("shard")) * own_count
    left_own = lax.dynamic_slice_in_dim(left_orth, first_row, own_count, 0)
    owned_rows = jnp.dot(left_own, right_full.T, precision=lax.Precision.HIGHEST)
    square_total = jnp.sum(right_full * right_full)
    grad_norm = jnp.sqrt(square_total)
    clip_level = CLIP_LEVEL * jnp.sqrt(jnp.float32(R * (D + F)))
    scaled = owned_rows * (clip_level / jnp.maximum(grad_norm, clip_level))
    first_out = BETA_ONE * first_moment + (1.0 - BETA_ONE) * scaled
    second_out = BETA_TWO * second_moment + (1.0 - BETA_TWO) * scaled * scaled
    direction = first_out / (jnp.sqrt(second_out) + EPSILON)
    return (error_out, first_out, second_out, direction)


def solution(mesh):
    return jax.shard_map(
        local,
        mesh=mesh,
        in_specs=(
            P("dp", None, "shard"),
            P("dp", None, "shard"),
            P("shard", None),
            P(("dp", "shard"), None),
            P(("dp", "shard"), None),
        ),
        out_specs=(
            P("dp", None, "shard"),
            P(("dp", "shard"), None),
            P(("dp", "shard"), None),
            P(("dp", "shard"), None),
        ),
        check_vma=False,
    )
```

profile of v0, /device:TPU:1, one launch (start us, length us, event | category | flops | bytes accessed | tf_op | source)
XLA Modules:
  0.0 137.0 jit_solution(12787354762281012879)
XLA Ops:
  0.6 0.0 copy-start.2
  0.6 3.7 %add_convert_fusion = bf16[1,4096,384]{2,1,0:T(8,128)(2,1)S(1)} fusion(bf16[1,4096,384]{2,1,0:T(8,128)(2,1)} %param.6, bf16[1,4096,384]{2,1,0:T(8,128)(2,1)} %param.5), kind=kLoop, calls=%fused_computation.2 | loop fusion | flops 6291456 | bytes 9437184 | tf_op jit(solution)/shard_map/convert_element_type | solution.py:62
  4.3 0.0 copy-done.2
  4.3 1.1 fusion.5
  5.4 27.2 %all_to_all.20 = f32[16,256,32]{1,2,0:T(8,128)} all-to-all(f32[16,256,32]{1,2,0:T(8,128)S(1)} %fusion.5), channel_id=1, replica_groups=mesh['dp'=16,'shard'=16] {'shard'}, dimensions={0} | all-to-all | bytes 1048576 | tf_op jit(solution)/shard_map/all_to_all | solution.py:25
  32.6 1.1 reduce_sum.46
  33.7 18.0 %all_to_all.21 = f32[16,256,32]{1,2,0:T(8,128)} all-to-all(f32[16,256,32]{1,2,0:T(8,128)S(1)} %broadcast_in_dim.14), channel_id=1, replica_groups=mesh['dp'=16,'shard'=16] {'dp'}, dimensions={0} | all-to-all | bytes 1048576 | tf_op jit(solution)/shard_map/all_to_all | solution.py:31
  51.7 1.1 reduce_sum.47
  52.8 15.9 %all_gather.3 = f32[4096,32]{0,1:T(8,128)S(1)} all-gather(f32[256,32]{0,1:T(8,128)S(1)} %broadcast_multiply_fusion.1), channel_id=1, replica_groups=mesh['dp'=16,'shard'=16] {'shard'}, dimensions={0}, use_global_device_ids=true | all-gather | bytes 557056 | tf_op jit(solution)/shard_map/all_gather | solution.py:69
  68.7 0.0 copy-start
  68.7 0.8 copy-done
  69.5 1.2 select_reduce_fusion.1
  70.6 0.1 copy.14
  71.4 2.9 %cholesky.17 = f32[32,32]{1,0:T(8,128)S(1)} custom-call(f32[32,32]{1,0:T(8,128)S(1)} %fusion.12), custom_call_target="Cholesky" | custom-call | tf_op jit(solution)/shard_map/jit(cholesky)/cholesky | solution.py:51
  74.3 0.6 compare_reduce_fusion
  75.0 0.7 fusion.8
  75.6 2.4 %custom-call.6 = f32[1,32,32]{1,2,0:T(8,128)S(1)} custom-call(f32[1,32,32]{2,1,0:T(8,128)S(1)} %fusion.8), custom_call_target="InvertDiagBlocksLowerTriangular" | custom-call | tf_op jit(solution)/shard_map/triangular_solve | solution.py:54
  78.0 1.7 %fusion.9 = f32[4096,32]{0,1:T(8,128)S(1)} fusion(f32[4096,32]{0,1:T(8,128)} %copy-done, f32[1,32,32]{1,2,0:T(8,128)S(1)} %custom-call.6), kind=kOutput, calls=%fused_computation.18 | convolution fusion | flops 50331648 | bytes 1052672 | tf_op jit(solution)/shard_map/triangular_solve | solution.py:54
  79.7 0.0 copy-start.1
  79.7 0.8 copy-done.1
  80.6 0.5 fusion.1
  81.1 0.1 broadcast_in_dim.16
  81.2 16.7 %all_to_all.22 = f32[16,384,32]{1,2,0:T(8,128)} all-to-all(f32[16,384,32]{1,2,0:T(8,128)S(1)} %broadcast_in_dim.16), channel_id=1, replica_groups=mesh['dp'=16,'shard'=16] {'dp'}, dimensions={0} | all-to-all | bytes 1572864 | tf_op jit(solution)/shard_map/all_to_all | solution.py:31
  97.9 1.2 reduce_sum.49
  99.1 1.0 broadcast_in_dim.31
  100.1 7.3 %all-to-all-start.3 = ((f32[16,384,32]{1,2,0:T(8,128)}), f32[16,384,32]{1,2,0:T(8,128)}, u32[]{:S(2)}, u32[]{:S(2)}) async-start(f32[16,384,32]{1,2,0:T(8,128)} %broadcast_in_dim.31), calls=%async_computation.3 | async-start | bytes 1572864 | tf_op jit(solution)/shard_map/all_to_all | solution.py:31
  107.4 7.8 %fusion = bf16[1,4096,384]{2,1,0:T(8,128)(2,1)} fusion(f32[4096,32]{0,1:T(8,128)} %copy-done.1, bf16[1,4096,384]{2,1,0:T(8,128)(2,1)S(1)} %add_convert_fusion, f32[384,32]{0,1:T(8,128)S(1)} %reduce_sum.49), kind=kOutput, calls=%fused_computation.3 | convolution fusion | flops 608710656 | bytes 6864896 | tf_op jit(solution)/shard_map/dot_general | solution.py:79
  115.2 15.0 %all-to-all-done.3 = f32[16,384,32]{1,2,0:T(8,128)} async-done(((f32[16,384,32]{1,2,0:T(8,128)}), f32[16,384,32]{1,2,0:T(8,128)}, u32[]{:S(2)}, u32[]{:S(2)}) %all-to-all-start.3) | async-done | bytes 786464 | tf_op jit(solution)/shard_map/all_to_all | solution.py:31
  130.2 1.9 %multiply_reduce_fusion = f32[]{:T(128)} fusion(f32[16,384,32]{1,2,0:T(8,128)} %all-to-all-done.3), kind=kLoop, calls=%fused_computation.6 | loop fusion | flops 393215 | bytes 786436 | tf_op jit(solution)/shard_map/reduce_sum | solution.py:87
  132.9 1.2 copy.16
  134.1 3.0 %add_divide_fusion = (f32[16,6144]{1,0:T(8,128)}, f32[16,6144]{1,0:T(8,128)}, f32[16,6144]{1,0:T(8,128)}) fusion(f32[16,6144]{1,0:T(8,128)} %param.9, f32[16,6144]{1,0:T(8,128)} %param.8, f32[]{:T(128)S(6)} %div.36, f32[6144,32]{0,1:T(8,128)S(1)} %bitcast.30, f32[4096,32]{0,1:T(8,128)} %copy-done.1, s32[]{:T(128)S(6)} %select_n.14), kind=kOutput, calls=%fused_computation.9 | convolution fusion | flops 38731776 | bytes 2768904 | tf_op jit(solution)/shard_map/dot_general | solution.py:86
  (5 shorter events, 0.1 us)
Async XLA Ops:
  0.6 3.7 %copy-start.2 = (f32[384,32]{0,1:T(8,128)S(1)}, f32[384,32]{0,1:T(8,128)}, u32[]{:S(2)}) copy-start(f32[384,32]{0,1:T(8,128)} %param.7) | copy-start | bytes 147460
  68.7 0.8 copy-start
  79.7 0.8 copy-start.1
  100.1 30.1 %all-to-all-start.3 = ((f32[16,384,32]{1,2,0:T(8,128)}), f32[16,384,32]{1,2,0:T(8,128)}, u32[]{:S(2)}, u32[]{:S(2)}) async-start(f32[16,384,32]{1,2,0:T(8,128)} %broadcast_in_dim.31), calls=%async_computation.3 | async-start | bytes 1572864 | tf_op jit(solution)/shard_map/all_to_all | solution.py:31
where the time goes:
time: 138 us; the launch traced here: 137 us
  blocking collectives  77.8 us (56%)
  other arithmetic  15.6 us (11%)
  matrix products  15.2 us (11%)
  waiting for transfers between devices  15 us (11%)
  starting transfers between devices  7.33 us (5%)
  local copies, waits for them, and re-layouts  3.97 us (3%)
  between operations  2.13 us (2%)
    all_to_all x2, blocking collectives, sent_to_all(): lax.all_to_all(jnp.broadcast_to(x[None], (count, *x.shape)), axis, 0, 0,...  34.7 us
    all_to_all x1, blocking collectives, sent_and_summed(): lax.all_to_all(tiles, axis, split_axis=0, concat_axis=0, tiled=True)  27.2 us
    all_gather x1, blocking collectives, local(): left_raw = lax.all_gather(row_share, 'shard', axis=0, tiled=True)  15.9 us
    all_to_all x1, waiting for transfers between devices, sent_to_all(): lax.all_to_all(jnp.broadcast_to(x[None], (count, *x.shape)), axis, 0, 0,...  15 us
    dot_general x1, matrix products, local(): update = jnp.dot(left_orth, right_mean.T, precision=lax.Precision.HIGHEST)  7.79 us
    all_to_all x1, starting transfers between devices, sent_to_all(): lax.all_to_all(jnp.broadcast_to(x[None], (count, *x.shape)), axis, 0, 0,...  7.33 us
    convert_element_type x1, other arithmetic, local(): (gradient[0].astype(jnp.float32) + error_buffer[0].astype(jnp.float32)).a...  3.66 us
    another operation x3, other arithmetic, orthonormal(): jnp.linalg.cholesky(gram_matrix + ridge_shift * jnp.eye(width, dtype=jnp....  3.59 us
  transfers between devices with their start and end apart: 1, of which 1 were waited for; matrix products, arithmetic and copies ran while one was open for 6% of the time, Pallas kernels for 0%

commit v1 on v0

v1 whole, which is shorter than its diff:
```python
import jax
import jax.numpy as jnp
from jax import lax
from jax.experimental import pallas as pl
from jax.experimental.pallas import tpu as pltpu
from jax.sharding import PartitionSpec as P

D = 4096
F = 6144
R = 32
DP = 16
SH = 16
ZN = 8
CHUNKS = 8
ROWS = D // CHUNKS
COLS = F // SH
OWN = D // (DP * SH)

CLIP_LEVEL = 0.9
BETA_ONE = 0.9
BETA_TWO = 0.95
EPSILON = 1e-08

MESH = pl.DeviceIdType.MESH
F32 = jnp.float32
BF16 = jnp.bfloat16
NT = (((1,), (1,)), ((), ()))
NN = (((1,), (0,)), ((), ()))


def mm(a, b, dims):
    return lax.dot_general(a, b, dims, preferred_element_type=F32)


def split(x):
    high = x.astype(BF16)
    rest = x - high.astype(F32)
    mid = rest.astype(BF16)
    low = (rest - mid.astype(F32)).astype(BF16)
    return high, mid, low


def gram(parts):
    stack = jnp.concatenate(parts, axis=0)
    full = mm(stack, stack, NT)
    n = len(parts)
    rows = sum(full[R * a : R * (a + 1)] for a in range(n))
    return sum(rows[:, R * a : R * (a + 1)] for a in range(n))


def triangular_inverse(gram_matrix):
    row = lax.broadcasted_iota(jnp.int32, (R, R), 0)
    col = lax.broadcasted_iota(jnp.int32, (R, R), 1)
    eye = row == col
    trace = jnp.sum(jnp.where(eye, gram_matrix, 0.0), keepdims=True)
    shifted = gram_matrix + jnp.where(eye, 1e-06 * trace / R, 0.0)
    work = jnp.concatenate([shifted, jnp.where(eye, 1.0, 0.0)], axis=1)
    wide_row = lax.broadcasted_iota(jnp.int32, (R, 2 * R), 0)
    wide_col = lax.broadcasted_iota(jnp.int32, (R, 2 * R), 1)
    for k in range(R - 1):
        column = jnp.broadcast_to(work[:, k : k + 1], (R, 2 * R))
        pivot = column[k : k + 1]
        line = work[k : k + 1] * (1.0 / pivot)
        work = work - jnp.where(wide_row > k, column, 0.0) * line
    diagonal = jnp.sum(jnp.where(wide_row == wide_col, work, 0.0), axis=1, keepdims=True)
    return work[:, R : 2 * R] * lax.rsqrt(diagonal)


def kernel(
    right_ref, grad_hbm, errb_hbm, first_hbm, second_hbm,
    err_hbm, first_out_hbm, second_out_hbm, direction_hbm,
    grad_buf, errb_buf, merged, part, core_in, half, dp_in, z_out, z_in, z_all, left_raw,
    left_split, left_stack, right_out, right_in, right_all, blocks, owned,
    first_buf, second_buf, first_res, second_res, direction_res,
    load_g, load_e, load_m,
    s_core, r_core, s_dp, r_dp, s_z, r_z, s_za, r_za, s_dpa, r_dpa, s_ca, r_ca,
    s_rr, r_rr, s_ra, r_ra, s_bz, r_bz, s_bc, r_bc, out_e, out_m,
):
    i = lax.axis_index("dp")
    j = lax.axis_index("shard")
    x, y = i // 4, i % 4
    z, c = j // 2, j % 2
    other = j + 1 - 2 * c

    def dp_peer(d):
        return ((x + d // 4) % 4) * 4 + (y + d % 4) % 4

    def z_peer(d):
        return (z + d) % ZN

    def remote(src, dst, ss, rs, dp, sh):
        return pltpu.make_async_remote_copy(
            src_ref=src, dst_ref=dst, send_sem=ss, recv_sem=rs, device_id=(dp, sh), device_id_type=MESH
        )

    barrier = pltpu.get_barrier_semaphore()

    loads = []
    for k in range(CHUNKS):
        chunk = (k + (CHUNKS // 2) * (1 - c)) % CHUNKS
        a = pltpu.make_async_copy(grad_hbm.at[chunk], grad_buf.at[chunk], load_g.at[k])
        b = pltpu.make_async_copy(errb_hbm.at[chunk], errb_buf.at[chunk], load_e.at[k])
        a.start()
        b.start()
        loads.append((chunk, a, b))
    for d in range(1, DP):
        pl.semaphore_signal(barrier, inc=1, device_id=(dp_peer(d), j), device_id_type=MESH)
    for d in range(1, ZN):
        pl.semaphore_signal(barrier, inc=1, device_id=(i, 2 * z_peer(d) + c), device_id_type=MESH)
    pl.semaphore_signal(barrier, inc=1, device_id=(i, other), device_id_type=MESH)
    load_first = pltpu.make_async_copy(first_hbm, first_buf, load_m.at[0])
    load_second = pltpu.make_async_copy(second_hbm, second_buf, load_m.at[1])

    right_low = right_ref[...].astype(BF16)
    sends = []
    for k in range(CHUNKS):
        chunk, a, b = loads[k]
        a.wait()
        b.wait()
        total = (grad_buf[chunk].astype(F32) + errb_buf[chunk].astype(F32)).astype(BF16)
        merged[chunk] = total
        product = mm(right_low, total, NT)
        for t in range(4):
            part[4 * chunk + t] = product[:, 128 * t : 128 * (t + 1)]
        if k == 0:
            pl.semaphore_wait(barrier, DP - 1 + ZN - 1 + 1)
        if k < CHUNKS // 2:
            copy = remote(
                part.at[pl.ds(4 * chunk, 4)], core_in.at[pl.ds(4 * k, 4)], s_core.at[k], r_core.at[k], i, other
            )
            copy.start()
            sends.append(copy)
        else:
            q = k - CHUNKS // 2
            remote(
                part.at[pl.ds(4 * chunk, 4)], core_in.at[pl.ds(4 * q, 4)], s_core.at[q], r_core.at[q], i, other
            ).wait_recv()
            for t in range(4):
                half[4 * q + t] = part[4 * chunk + t] + core_in[4 * q + t]
    load_first.start()
    load_second.start()

    for d in range(1, DP):
        p = dp_peer(d)
        copy = remote(half.at[p], dp_in.at[i], s_dp.at[d], r_dp.at[i], p, j)
        copy.start()
        sends.append(copy)
    dp_in[i] = half[i]
    for d in range(1, DP):
        p = dp_peer(d)
        remote(half.at[p], dp_in.at[p], s_dp.at[d], r_dp.at[p], p, j).wait_recv()
    total = dp_in[0]
    for p in range(1, DP):
        total = total + dp_in[p]
    for k in range(ZN):
        z_out[k] = total[4 * k : 4 * (k + 1)]
    for d in range(1, ZN):
        p = z_peer(d)
        copy = remote(z_out.at[p], z_in.at[z], s_z.at[d], r_z.at[z], i, 2 * p + c)
        copy.start()
        sends.append(copy)
    z_in[z] = z_out[z]
    for d in range(1, ZN):
        p = z_peer(d)
        remote(z_out.at[p], z_in.at[p], s_z.at[d], r_z.at[p], i, 2 * p + c).wait_recv()
    total = z_in[0]
    for p in range(1, ZN):
        total = total + z_in[p]
    z_all[z] = total * (1.0 / DP)

    for d in range(1, ZN):
        p = z_peer(d)
        copy = remote(z_all.at[z], z_all.at[z], s_za.at[d], r_za.at[z], i, 2 * p + c)
        copy.start()
        sends.append(copy)
    for d in range(1, ZN):
        p = z_peer(d)
        remote(z_all.at[p], z_all.at[p], s_za.at[d], r_za.at[p], i, 2 * p + c).wait_recv()
    mine = DP * c + i
    for k in range(ZN):
        left_raw[mine, pl.ds(4 * k, 4), :] = z_all[k]
    for d in range(1, DP):
        p = dp_peer(d)
        copy = remote(left_raw.at[mine], left_raw.at[mine], s_dpa.at[d], r_dpa.at[i], p, j)
        copy.start()
        sends.append(copy)
    copy = remote(left_raw.at[mine], left_raw.at[mine], s_ca.at[i], r_ca.at[i], i, other)
    copy.start()
    sends.append(copy)
    for d in range(1, DP):
        p = dp_peer(d)
        q = DP * c + p
        remote(left_raw.at[q], left_raw.at[q], s_dpa.at[d], r_dpa.at[p], p, j).wait_recv()
        copy = remote(left_raw.at[q], left_raw.at[q], s_ca.at[p], r_ca.at[p], i, other)
        copy.start()
        sends.append(copy)
    for p in range(DP):
        q = DP * (1 - c) + p
        remote(left_raw.at[q], left_raw.at[q], s_ca.at[p], r_ca.at[p], i, other).wait_recv()

    gram_matrix = jnp.zeros((R, R), F32)
    for k in range(CHUNKS):
        wide = jnp.concatenate([left_raw[4 * k + t] for t in range(4)], axis=1)
        parts = split(wide)
        for n in range(3):
            left_split[k, n] = parts[n]
        gram_matrix = gram_matrix + gram(parts)
    inverse = split(triangular_inverse(gram_matrix))
    inverse = jnp.concatenate([jnp.concatenate([t] * 3, axis=1) for t in inverse], axis=0)

    right_part = jnp.zeros((R, COLS), F32)
    for k in range(CHUNKS):
        stack = jnp.concatenate([left_split[k, n] for n in range(3)], axis=0)
        wide = mm(inverse, stack, NN)
        parts = split(wide[:R] + wide[R : 2 * R] + wide[2 * R :])
        for n in range(3):
            left_split[k, n] = parts[n]
        right_part = right_part + mm(parts[0], merged[k], NN)
    for p in range(DP):
        right_out[p] = right_part[2 * p : 2 * p + 2]
    for d in range(1, DP):
        p = dp_peer(d)
        copy = remote(right_out.at[p], right_in.at[i], s_rr.at[d], r_rr.at[i], p, j)
        copy.start()
        sends.append(copy)
    right_in[i] = right_out[i]
    ortho_gram = jnp.zeros((R, R), F32)
    for k in range(CHUNKS):
        high, mid, low = (left_split[k, n] for n in range(3))
        ortho_gram = ortho_gram + gram((high, mid, low))
        left_stack[k] = jnp.concatenate([high, high, mid, mid], axis=0).T
    for d in range(1, DP):
        p = dp_peer(d)
        remote(right_out.at[p], right_in.at[p], s_rr.at[d], r_rr.at[p], p, j).wait_recv()
    total = right_in[0]
    for p in range(1, DP):
        total = total + right_in[p]
    right_all[i] = total * (1.0 / DP)
    for d in range(1, DP):
        p = dp_peer(d)
        copy = remote(right_all.at[i], right_all.at[i], s_ra.at[d], r_ra.at[i], p, j)
        copy.start()
        sends.append(copy)
    for d in range(1, DP):
        p = dp_peer(d)
        remote(right_all.at[p], right_all.at[p], s_ra.at[d], r_ra.at[p], p, j).wait_recv()
    for p in range(DP):
        blocks[j, pl.ds(2 * p, 2), :] = right_all[p]

    for d in range(1, ZN):
        p = z_peer(d)
        copy = remote(blocks.at[j], blocks.at[j], s_bz.at[d], r_bz.at[z], i, 2 * p + c)
        copy.start()
        sends.append(copy)
    copy = remote(blocks.at[j], blocks.at[j], s_bc.at[z], r_bc.at[z], i, other)
    copy.start()
    sends.append(copy)

    high, mid, low = split(blocks[j])
    mine_stack = jnp.concatenate([high, mid, high, mid], axis=0)
    outs = []
    for k in range(CHUNKS):
        update = mm(left_stack[k], mine_stack, NN)
        errb_buf[k] = (merged[k].astype(F32) - update).astype(BF16)
        copy = pltpu.make_async_copy(errb_buf.at[k], err_hbm.at[k], out_e.at[k])
        copy.start()
        outs.append(copy)
        if k > 0:
            p = z_peer(k)
            q = 2 * p + c
            remote(blocks.at[q], blocks.at[q], s_bz.at[k], r_bz.at[p], i, q).wait_recv()
            copy = remote(blocks.at[q], blocks.at[q], s_bc.at[p], r_bc.at[p], i, other)
            copy.start()
            sends.append(copy)
    for p in range(ZN):
        q = 2 * p + 1 - c
        remote(blocks.at[q], blocks.at[q], s_bc.at[p], r_bc.at[p], i, other).wait_recv()

    tile = 2 * i + j // 8
    first_lane = OWN * (j % 8)
    pick = (
        lax.broadcasted_iota(jnp.int32, (OWN, 128), 1) == lax.broadcasted_iota(jnp.int32, (OWN, 128), 0) + first_lane
    )
    pick = jnp.where(pick, 1.0, 0.0).astype(BF16)
    lane_tile = tile % 4
    chunk = tile // 4
    own = []
    for n in range(2):
        whole = left_split[chunk, n]
        rows = mm(pick, whole[:, 0:128], NT) * jnp.where(lane_tile == 0, 1.0, 0.0)
        for t in range(1, 4):
            rows = rows + mm(pick, whole[:, 128 * t : 128 * (t + 1)], NT) * jnp.where(lane_tile == t, 1.0, 0.0)
        own.append(rows.astype(BF16))
    own_stack = jnp.concatenate([own[0], own[0], own[1], own[1]], axis=1)
    square = jnp.zeros((R, R), F32)
    for q in range(SH):
        high, mid, low = split(blocks[q])
        square = square + gram((high, mid))
        owned[:, COLS * q : COLS * (q + 1)] = mm(own_stack, jnp.concatenate([high, mid, high, mid], axis=0), NN)
    norm = jnp.sqrt(jnp.sum(square * ortho_gram, keepdims=True))
    clip_level = CLIP_LEVEL * (float(R * (D + F)) ** 0.5)
    scale = clip_level / jnp.maximum(norm, clip_level)
    load_first.wait()
    load_second.wait()
    for q in range(SH):
        lanes = slice(COLS * q, COLS * (q + 1))
        scaled = owned[:, lanes] * scale
        first = BETA_ONE * first_buf[:, lanes] + (1.0 - BETA_ONE) * scaled
        second = BETA_TWO * second_buf[:, lanes] + (1.0 - BETA_TWO) * scaled * scaled
        first_res[:, lanes] = first
        second_res[:, lanes] = second
        direction_res[:, lanes] = first / (jnp.sqrt(second) + EPSILON)
    for n, (res, hbm) in enumerate(
        ((first_res, first_out_hbm), (second_res, second_out_hbm), (direction_res, direction_hbm))
    ):
        copy = pltpu.make_async_copy(res, hbm, out_m.at[n])
        copy.start()
        outs.append(copy)
    for copy in sends:
        copy.wait_send()
    for copy in outs:
        copy.wait()


def local(gradient, error_buffer, right_init, first_moment, second_moment):
    shape3 = (CHUNKS, ROWS, COLS)
    dma = pltpu.SemaphoreType.DMA
    vmem = pltpu.VMEM
    err, first, second, direction = pl.pallas_call(
        kernel,
        out_shape=(
            jax.ShapeDtypeStruct(shape3, BF16),
            jax.ShapeDtypeStruct((OWN, F), F32),
            jax.ShapeDtypeStruct((OWN, F), F32),
            jax.ShapeDtypeStruct((OWN, F), F32),
        ),
        in_specs=[pl.BlockSpec(memory_space=pltpu.VMEM)] + [pl.BlockSpec(memory_space=pltpu.HBM)] * 4,
        out_specs=(pl.BlockSpec(memory_space=pl.ANY),) * 4,
        scratch_shapes=[
            vmem(shape3, BF16),
            vmem(shape3, BF16),
            vmem(shape3, BF16),
            vmem((2 * DP, R, 128), F32),
            vmem((DP, R, 128), F32),
            vmem((DP, R, 128), F32),
            vmem((DP, R, 128), F32),
            vmem((ZN, 4, 128), F32),
            vmem((ZN, 4, 128), F32),
            vmem((ZN, 4, 128), F32),
            vmem((2 * DP, R, 128), F32),
            vmem((CHUNKS, 3, R, ROWS), BF16),
            vmem((CHUNKS, ROWS, 128), BF16),
            vmem((DP, 2, COLS), F32),
            vmem((DP, 2, COLS), F32),
            vmem((DP, 2, COLS), F32),
            vmem((SH, R, COLS), F32),
            vmem((OWN, F), F32),
            vmem((OWN, F), F32),
            vmem((OWN, F), F32),
            vmem((OWN, F), F32),
            vmem((OWN, F), F32),
            vmem((OWN, F), F32),
            dma((CHUNKS,)), dma((CHUNKS,)), dma((2,)),
            dma((4,)), dma((4,)),
            dma((DP,)), dma((DP,)),
            dma((ZN,)), dma((ZN,)),
            dma((ZN,)), dma((ZN,)),
            dma((DP,)), dma((DP,)),
            dma((DP,)), dma((DP,)),
            dma((DP,)), dma((DP,)),
            dma((DP,)), dma((DP,)),
            dma((ZN,)), dma((ZN,)),
            dma((ZN,)), dma((ZN,)),
            dma((CHUNKS,)), dma((3,)),
        ],
        compiler_params=pltpu.CompilerParams(
            collective_id=0, has_side_effects=True, vmem_limit_bytes=28 * 1024 * 1024
        ),
    )(
        right_init.T,
        gradient.reshape(shape3),
        error_buffer.reshape(shape3),
        first_moment,
        second_moment,
    )
    return (err.reshape(1, D, COLS), first, second, direction)


def solution(mesh):
    return jax.shard_map(
        local,
        mesh=mesh,
        in_specs=(
            P("dp", None, "shard"),
            P("dp", None, "shard"),
            P("shard", None),
            P(("dp", "shard"), None),
            P(("dp", "shard"), None),
        ),
        out_specs=(
            P("dp", None, "shard"),
            P(("dp", "shard"), None),
            P(("dp", "shard"), None),
            P(("dp", "shard"), None),
        ),
        check_vma=False,
    )
```

time: 138 us -> 81.9 us (0.59)
  blocking collectives: 77.8 us -> 0 us
  Pallas kernels: 0 us -> 70.5 us
  other arithmetic: 15.6 us -> 0 us
  matrix products: 15.2 us -> 0 us
  waiting for transfers between devices: 15 us -> 0 us
  starting transfers between devices: 7.33 us -> 0 us
  local copies, waits for them, and re-layouts: 3.97 us -> 10.5 us
  between operations: 2.13 us -> 0.65 us
    pallas_call x0 -> x1, Pallas kernels: none -> 70.5 us  [local(): pl.pallas_call(kernel, out_shape=(jax.ShapeDtypeStruct(shape3, BF16), jax...]
    all_to_all x3 -> x0, blocking collectives: 61.9 us -> none  [the longest x2 34.7 us: sent_to_all(): lax.all_to_all(jnp.broadcast_to(x[None], (count, *x.shape)), axis, 0, 0,...]
    all_gather x1 -> x0, blocking collectives: 15.9 us -> none  [local(): left_raw = lax.all_gather(row_share, 'shard', axis=0, tiled=True)]
    all_to_all x1 -> x0, waiting for transfers between devices: 15 us -> none  [sent_to_all(): lax.all_to_all(jnp.broadcast_to(x[None], (count, *x.shape)), axis, 0, 0,...]
    dot_general x5 -> x0, matrix products: 13.5 us -> none  [the longest x1 7.79 us: local(): update = jnp.dot(left_orth, right_mean.T, precision=lax.Precision.HIGHEST)]
    unnamed x6 -> x14, local copies, waits for them, and re-layouts: 1.6 us -> 10.5 us
    all_to_all x1 -> x0, starting transfers between devices: 7.33 us -> none  [sent_to_all(): lax.all_to_all(jnp.broadcast_to(x[None], (count, *x.shape)), axis, 0, 0,...]
    another operation x5 -> x0, other arithmetic: 6.67 us -> none  [the longest x3 3.59 us: orthonormal(): jnp.linalg.cholesky(gram_matrix + ridge_shift * jnp.eye(width, dtype=jnp....]
  transfers between devices with their start and end apart: 1 -> 0, of which waited for: 1 -> 0; matrix products, arithmetic and copies ran while one was open for 6% -> 0% of each run, Pallas kernels for 0% -> 0%
where the time goes in v1:
time: 81.9 us; the launch traced here: 81.6 us
  Pallas kernels  70.5 us (86%)
  local copies, waits for them, and re-layouts  10.5 us (13%)
    pallas_call x1, Pallas kernels, local(): pl.pallas_call(kernel, out_shape=(jax.ShapeDtypeStruct(shape3, BF16), jax...  70.5 us
    unnamed x14, local copies, waits for them, and re-layouts  10.5 us

profile of v1, /device:TPU:1, one launch (start us, length us, event | category | flops | bytes accessed | tf_op | source)
XLA Modules:
  0.0 81.6 jit_solution(17129731861344802363)
XLA Ops:
  0.6 0.0 copy-start
  0.6 1.9 %copy-done = bf16[1,4096,384]{2,1,0:T(8,128)(2,1)S(1)} copy-done((bf16[1,4096,384]{2,1,0:T(8,128)(2,1)S(1)}, bf16[1,4096,384]{2,1,0:T(8,128)(2,1)}, u32[]{:S(2)}) %copy-start) | copy-done | bytes 3145752
  2.5 0.0 copy-start.1
  2.5 1.9 %copy-done.1 = bf16[1,4096,384]{2,1,0:T(8,128)(2,1)S(1)} copy-done((bf16[1,4096,384]{2,1,0:T(8,128)(2,1)S(1)}, bf16[1,4096,384]{2,1,0:T(8,128)(2,1)}, u32[]{:S(2)}) %copy-start.1) | copy-done | bytes 3145752
  4.4 0.0 copy-start.2
  4.4 1.0 %copy-done.2 = f32[16,6144]{1,0:T(8,128)S(1)} copy-done((f32[16,6144]{1,0:T(8,128)S(1)}, f32[16,6144]{1,0:T(8,128)}, u32[]{:S(2)}) %copy-start.2) | copy-done | bytes 393240
  5.4 0.0 copy-start.3
  5.4 1.0 %copy-done.3 = f32[16,6144]{1,0:T(8,128)S(1)} copy-done((f32[16,6144]{1,0:T(8,128)S(1)}, f32[16,6144]{1,0:T(8,128)}, u32[]{:S(2)}) %copy-start.3) | copy-done | bytes 393240
  6.4 0.0 copy-start.4
  6.4 0.8 copy-done.4
  7.2 70.5 %shard_map.84 = (bf16[8,512,384]{2,1,0:T(8,128)(2,1)S(1)}, f32[16,6144]{1,0:T(8,128)S(1)}, f32[16,6144]{1,0:T(8,128)S(1)}, f32[16,6144]{1,0:T(8,128)S(1)}) custom-call(f32[32,384]{1,0:T(8,128)S(1)} %bitcast.7, bf16[8,512,384]{2,1,0:T(8,128)(2,1)S(1)} %bitcast.4, bf16[8,512,384]{2,1,0:T(8,128)(2,1)S(1)} %bitcast.5, f32[16,6144]{1,0:T(8,128)S(1)} %copy-done.2, ...), custom_call_target="tpu_custom_call" | custom-call | tf_op jit(solution)/shard_map/pallas_call | solution.py:329
  77.7 1.7 %copy.13 = bf16[1,4096,384]{2,1,0:T(8,128)(2,1)} copy(bf16[1,4096,384]{2,1,0:T(8,128)(2,1)S(1)} %bitcast.6) | data formatting | bytes 6291456
  79.3 0.7 copy.14
  80.1 0.7 copy.15
  80.8 0.7 copy.16
Async XLA Ops:
  0.6 1.9 %copy-start = (bf16[1,4096,384]{2,1,0:T(8,128)(2,1)S(1)}, bf16[1,4096,384]{2,1,0:T(8,128)(2,1)}, u32[]{:S(2)}) copy-start(bf16[1,4096,384]{2,1,0:T(8,128)(2,1)} %param.5) | copy-start | bytes 9437188
  2.5 1.9 %copy-start.1 = (bf16[1,4096,384]{2,1,0:T(8,128)(2,1)S(1)}, bf16[1,4096,384]{2,1,0:T(8,128)(2,1)}, u32[]{:S(2)}) copy-start(bf16[1,4096,384]{2,1,0:T(8,128)(2,1)} %param.6) | copy-start | bytes 9437188
  4.4 1.0 %copy-start.2 = (f32[16,6144]{1,0:T(8,128)S(1)}, f32[16,6144]{1,0:T(8,128)}, u32[]{:S(2)}) copy-start(f32[16,6144]{1,0:T(8,128)} %first_hbm.1) | copy-start | bytes 1179652
  5.4 1.0 %copy-start.3 = (f32[16,6144]{1,0:T(8,128)S(1)}, f32[16,6144]{1,0:T(8,128)}, u32[]{:S(2)}) copy-start(f32[16,6144]{1,0:T(8,128)} %second_hbm.1) | copy-start | bytes 1179652
  6.4 0.8 copy-start.4

commit v2 on v0

v2 whole, which is shorter than its diff:
```python
import jax
import jax.numpy as jnp
from jax import lax
from jax.experimental import pallas as pl
from jax.experimental.pallas import tpu as pltpu
from jax.sharding import PartitionSpec as P

D = 4096
F = 6144
R = 32
DP = 16
SH = 16
ZN = 8
CHUNKS = 8
ROWS = D // CHUNKS
COLS = F // SH
OWN = D // (DP * SH)

CLIP_LEVEL = 0.9
BETA_ONE = 0.9
BETA_TWO = 0.95
EPSILON = 1e-08

MESH = pl.DeviceIdType.MESH
F32 = jnp.float32
BF16 = jnp.bfloat16
NT = (((1,), (1,)), ((), ()))
NN = (((1,), (0,)), ((), ()))


def mm(a, b, dims):
    return lax.dot_general(a, b, dims, preferred_element_type=F32)


def split(x):
    high = x.astype(BF16)
    rest = x - high.astype(F32)
    mid = rest.astype(BF16)
    low = (rest - mid.astype(F32)).astype(BF16)
    return high, mid, low


def fold(full, n):
    rows = sum(full[R * a : R * (a + 1)] for a in range(n))
    return sum(rows[:, R * a : R * (a + 1)] for a in range(n))


def triangular_inverse(gram_matrix):
    row = lax.broadcasted_iota(jnp.int32, (R, R), 0)
    col = lax.broadcasted_iota(jnp.int32, (R, R), 1)
    eye = row == col
    trace = jnp.sum(jnp.where(eye, gram_matrix, 0.0), keepdims=True)
    shifted = gram_matrix + jnp.where(eye, 1e-06 * trace / R, 0.0)
    work = jnp.concatenate([shifted, jnp.where(eye, 1.0, 0.0)], axis=1)
    wide_row = lax.broadcasted_iota(jnp.int32, (R, 2 * R), 0)
    wide_col = lax.broadcasted_iota(jnp.int32, (R, 2 * R), 1)
    for k in range(R - 1):
        column = jnp.broadcast_to(work[:, k : k + 1], (R, 2 * R))
        pivot = column[k : k + 1]
        line = work[k : k + 1] * (1.0 / pivot)
        work = work - jnp.where(wide_row > k, column, 0.0) * line
    diagonal = jnp.sum(jnp.where(wide_row == wide_col, work, 0.0), axis=1, keepdims=True)
    return work[:, R : 2 * R] * lax.rsqrt(diagonal)


def kernel(
    right_hbm, grad_hbm, errb_hbm,
    err_ref, scaled_ref,
    right_buf, grad_buf, errb_buf, merged, part, core_in, half, dp_in, z_in, left_raw,
    left_split, left_stack, right_out, right_in, right_all, right_raw, blocks,
    load_g, load_e, load_m,
    s_core, r_core, s_dp, r_dp, s_z, r_z, s_dpa, r_dpa, s_ca, r_ca,
    s_rr, r_rr, s_ra, r_ra, s_bz, r_bz, s_bc, r_bc,
):
    i = lax.axis_index("dp")
    j = lax.axis_index("shard")
    x, y = i // 4, i % 4
    z, c = j // 2, j % 2
    other = j + 1 - 2 * c

    def dp_peer(d):
        return ((x + d // 4) % 4) * 4 + (y + d % 4) % 4

    def z_peer(d):
        return (z + d) % ZN

    def hops(d):
        return min(d // 4, 4 - d // 4) + min(d % 4, 4 - d % 4)

    dp_near = sorted(range(1, DP), key=hops)
    dp_far = dp_near[::-1]
    z_near = sorted(range(1, ZN), key=lambda d: min(d, ZN - d))
    z_far = z_near[::-1]

    def remote(src, dst, ss, rs, dp, sh):
        return pltpu.make_async_remote_copy(
            src_ref=src, dst_ref=dst, send_sem=ss, recv_sem=rs, device_id=(dp, sh), device_id_type=MESH
        )

    sends = []
    loads = []

    def send(*args):
        copy = remote(*args)
        copy.start()
        sends.append(copy)

    def finish():
        for copy in sends:
            copy.wait_send()

    barrier = pltpu.get_barrier_semaphore()
    for d in dp_far:
        pl.semaphore_signal(barrier, inc=1, device_id=(dp_peer(d), j), device_id_type=MESH)
    for d in z_far:
        pl.semaphore_signal(barrier, inc=1, device_id=(i, 2 * z_peer(d) + c), device_id_type=MESH)
    pl.semaphore_signal(barrier, inc=1, device_id=(i, other), device_id_type=MESH)
    load_right = pltpu.make_async_copy(right_hbm, right_buf, load_m)
    load_right.start()
    for k in range(CHUNKS):
        a = pltpu.make_async_copy(grad_hbm.at[k], grad_buf.at[k], load_g.at[k])
        b = pltpu.make_async_copy(errb_hbm.at[k], errb_buf.at[k], load_e.at[k])
        a.start()
        b.start()
        loads.append((a, b))

    load_right.wait()
    right_low = right_buf[...].astype(BF16)
    for k in range(CHUNKS):
        for copy in loads[k]:
            copy.wait()
        total = (grad_buf[k].astype(F32) + errb_buf[k].astype(F32)).astype(BF16)
        merged[4 * k : 4 * (k + 1)] = total.reshape(4, 128, COLS)
        product = mm(right_low, total, NT)
        for t in range(4):
            part[4 * k + t] = product[:, 128 * t : 128 * (t + 1)]

    pl.semaphore_wait(barrier, DP - 1 + ZN - 1 + 1)
    for k in range(4):
        send(part.at[pl.ds(DP * (1 - c) + 4 * k, 4)], core_in.at[pl.ds(4 * k, 4)], s_core.at[k], r_core.at[k], i, other)
    for k in range(4):
        remote(
            part.at[pl.ds(DP * c + 4 * k, 4)], core_in.at[pl.ds(4 * k, 4)], s_core.at[k], r_core.at[k], i, other
        ).wait_recv()
        for t in range(4 * k, 4 * k + 4):
            half[t] = part[DP * c + t] + core_in[t]
    for d in dp_far:
        p = dp_peer(d)
        send(half.at[p], dp_in.at[i], s_dp.at[d], r_dp.at[i], p, j)
    dp_in[i] = half[i]
    for d in dp_near:
        p = dp_peer(d)
        remote(half.at[p], dp_in.at[p], s_dp.at[d], r_dp.at[p], p, j).wait_recv()
    total = dp_in[0]
    for p in range(1, DP):
        total = total + dp_in[p]
    z_in[z] = total
    for d in z_far:
        p = z_peer(d)
        send(z_in.at[z], z_in.at[z], s_z.at[d], r_z.at[z], i, 2 * p + c)
    for d in z_near:
        p = z_peer(d)
        remote(z_in.at[p], z_in.at[p], s_z.at[d], r_z.at[p], i, 2 * p + c).wait_recv()
    total = z_in[0]
    for p in range(1, ZN):
        total = total + z_in[p]
    mine = DP * c + i
    left_raw[mine] = total * (1.0 / DP)
    for d in dp_far:
        send(left_raw.at[mine], left_raw.at[mine], s_dpa.at[d], r_dpa.at[i], dp_peer(d), j)
    send(left_raw.at[mine], left_raw.at[mine], s_ca.at[i], r_ca.at[i], i, other)
    for d in dp_near:
        p = dp_peer(d)
        q = DP * c + p
        remote(left_raw.at[q], left_raw.at[q], s_dpa.at[d], r_dpa.at[p], p, j).wait_recv()
        send(left_raw.at[q], left_raw.at[q], s_ca.at[p], r_ca.at[p], i, other)
    gram_sum = jnp.zeros((3 * R, 3 * R), F32)
    right_sum = jnp.zeros((3 * R, COLS), F32)
    for k in range(CHUNKS):
        if k < 4:
            first = DP * c + 4 * k
        else:
            first = DP * (1 - c) + 4 * (k - 4)
            for p in range(4 * (k - 4), 4 * (k - 3)):
                q = DP * (1 - c) + p
                remote(left_raw.at[q], left_raw.at[q], s_ca.at[p], r_ca.at[p], i, other).wait_recv()
        wide = jnp.concatenate([left_raw[first + t] for t in range(4)], axis=1)
        stack = jnp.concatenate(split(wide), axis=0)
        left_split[first // 4] = stack
        gram_sum = gram_sum + mm(stack, stack, NT)
        right_sum = right_sum + mm(stack, merged[pl.ds(first, 4)].reshape(ROWS, COLS), NN)
    right_part = right_sum[:R] + right_sum[R : 2 * R] + right_sum[2 * R :]
    for p in range(DP):
        right_out[p] = right_part[2 * p : 2 * p + 2]
    for d in dp_far:
        p = dp_peer(d)
        send(right_out.at[p], right_in.at[i], s_rr.at[d], r_rr.at[i], p, j)
    right_in[i] = right_out[i]
    inverse = split(triangular_inverse(fold(gram_sum, 3)))
    inverse = jnp.concatenate([jnp.concatenate([t] * 3, axis=1) for t in inverse], axis=0)
    for d in dp_near:
        p = dp_peer(d)
        remote(right_out.at[p], right_in.at[p], s_rr.at[d], r_rr.at[p], p, j).wait_recv()
    total = right_in[0]
    for p in range(1, DP):
        total = total + right_in[p]
    right_all[i] = total * (1.0 / DP)
    for d in dp_far:
        send(right_all.at[i], right_all.at[i], s_ra.at[d], r_ra.at[i], dp_peer(d), j)
    ortho_sum = jnp.zeros((2 * R, 2 * R), F32)
    for k in range(CHUNKS):
        wide = mm(inverse, left_split[k], NN)
        high, mid, _ = split(wide[:R] + wide[R : 2 * R] + wide[2 * R :])
        stack = jnp.concatenate([high, mid], axis=0)
        ortho_sum = ortho_sum + mm(stack, stack, NT)
        left_stack[32 * k : 32 * (k + 1)] = jnp.concatenate([high, high, mid, mid], axis=0).T.reshape(32, OWN, 128)
    ortho_gram = fold(ortho_sum, 2)
    for d in dp_near:
        p = dp_peer(d)
        remote(right_all.at[p], right_all.at[p], s_ra.at[d], r_ra.at[p], p, j).wait_recv()
    for p in range(DP):
        right_raw[2 * p : 2 * p + 2] = right_all[p]
    wide = mm(inverse, jnp.concatenate(split(right_raw[...]), axis=0), NN)
    blocks[j] = wide[:R] + wide[R : 2 * R] + wide[2 * R :]
    for d in z_far:
        send(blocks.at[j], blocks.at[j], s_bz.at[d], r_bz.at[z], i, 2 * z_peer(d) + c)
    send(blocks.at[j], blocks.at[j], s_bc.at[z], r_bc.at[z], i, other)
    own = left_stack[DP * i + j]

    def stacked(block):
        high, mid, _ = split(block)
        return jnp.concatenate([high, mid, high, mid], axis=0)

    mine_stack = stacked(blocks[j])
    for k in range(CHUNKS):
        rows = left_stack[32 * k : 32 * (k + 1)].reshape(ROWS, 128)
        whole = merged[4 * k : 4 * (k + 1)].reshape(ROWS, COLS)
        err_ref[k] = (whole.astype(F32) - mm(rows, mine_stack, NN)).astype(BF16)
    for d in z_near:
        p = z_peer(d)
        q = 2 * p + c
        remote(blocks.at[q], blocks.at[q], s_bz.at[d], r_bz.at[p], i, q).wait_recv()
        send(blocks.at[q], blocks.at[q], s_bc.at[p], r_bc.at[p], i, other)
    for p in range(ZN):
        q = 2 * p + 1 - c
        remote(blocks.at[q], blocks.at[q], s_bc.at[p], r_bc.at[p], i, other).wait_recv()
    square = jnp.zeros((2 * R, 2 * R), F32)
    rows = []
    for q in range(SH):
        stack = stacked(blocks[q])
        square = square + mm(stack[: 2 * R], stack[: 2 * R], NT)
        rows.append(mm(own, stack, NN))
    norm = jnp.sqrt(jnp.sum(fold(square, 2) * ortho_gram, keepdims=True))
    clip_level = CLIP_LEVEL * (float(R * (D + F)) ** 0.5)
    scale = clip_level / jnp.maximum(norm, clip_level)
    for q in range(SH):
        scaled_ref[:, COLS * q : COLS * (q + 1)] = rows[q] * scale
    finish()


def step_kernel(
    err_ref, scaled_ref, first_ref, second_ref, err_hbm, first_hbm, second_hbm, direction_hbm,
    first_res, second_res, direction_res, out_e, out_m,
):
    outs = [pltpu.make_async_copy(err_ref, err_hbm, out_e)]
    outs[0].start()
    pieces = 4
    width = F // pieces
    for q in range(pieces):
        lanes = pl.ds(width * q, width)
        scaled = scaled_ref[:, lanes]
        first = BETA_ONE * first_ref[:, lanes] + (1.0 - BETA_ONE) * scaled
        second = BETA_TWO * second_ref[:, lanes] + (1.0 - BETA_TWO) * scaled * scaled
        first_res[:, lanes] = first
        second_res[:, lanes] = second
        direction_res[:, lanes] = first / (jnp.sqrt(second) + EPSILON)
        for n, (res, hbm) in enumerate(
            ((first_res, first_hbm), (second_res, second_hbm), (direction_res, direction_hbm))
        ):
            copy = pltpu.make_async_copy(res.at[:, lanes], hbm.at[:, lanes], out_m.at[n, q])
            copy.start()
            outs.append(copy)
    for copy in outs:
        copy.wait()


def local(gradient, error_buffer, right_init, first_moment, second_moment):
    shape3 = (CHUNKS, ROWS, COLS)
    dma = pltpu.SemaphoreType.DMA
    vmem = pltpu.VMEM
    err, scaled = pl.pallas_call(
        kernel,
        out_shape=(jax.ShapeDtypeStruct(shape3, BF16), jax.ShapeDtypeStruct((OWN, F), F32)),
        in_specs=[pl.BlockSpec(memory_space=pltpu.HBM)] * 3,
        out_specs=(pl.BlockSpec(memory_space=pltpu.VMEM),) * 2,
        scratch_shapes=[
            vmem((R, COLS), F32),
            vmem(shape3, BF16),
            vmem(shape3, BF16),
            vmem((2 * DP, 128, COLS), BF16),
            vmem((2 * DP, R, 128), F32),
            vmem((DP, R, 128), F32),
            vmem((DP, R, 128), F32),
            vmem((DP, R, 128), F32),
            vmem((ZN, R, 128), F32),
            vmem((2 * DP, R, 128), F32),
            vmem((CHUNKS, 3 * R, ROWS), BF16),
            vmem((DP * SH, OWN, 128), BF16),
            vmem((DP, 2, COLS), F32),
            vmem((DP, 2, COLS), F32),
            vmem((DP, 2, COLS), F32),
            vmem((R, COLS), F32),
            vmem((SH, R, COLS), F32),
            dma((CHUNKS,)), dma((CHUNKS,)), dma(()),
            dma((4,)), dma((4,)),
            dma((DP,)), dma((DP,)),
            dma((ZN,)), dma((ZN,)),
            dma((DP,)), dma((DP,)),
            dma((DP,)), dma((DP,)),
            dma((DP,)), dma((DP,)),
            dma((DP,)), dma((DP,)),
            dma((ZN,)), dma((ZN,)),
            dma((ZN,)), dma((ZN,)),
        ],
        compiler_params=pltpu.CompilerParams(
            collective_id=0, has_side_effects=True, vmem_limit_bytes=28 * 1024 * 1024
        ),
    )(
        *(
            pltpu.with_memory_space_constraint(t, pltpu.HBM)
            for t in (right_init.T, gradient.reshape(shape3), error_buffer.reshape(shape3))
        )
    )
    own = jax.ShapeDtypeStruct((OWN, F), F32)
    err, first, second, direction = pl.pallas_call(
        step_kernel,
        out_shape=(jax.ShapeDtypeStruct(shape3, BF16), own, own, own),
        in_specs=[pl.BlockSpec(memory_space=pl.ANY)] + [pl.BlockSpec(memory_space=pltpu.VMEM)] * 3,
        out_specs=(pl.BlockSpec(memory_space=pltpu.HBM),) * 4,
        scratch_shapes=[
            vmem((OWN, F), F32), vmem((OWN, F), F32), vmem((OWN, F), F32),
            dma(()), dma((3, 4)),
        ],
        compiler_params=pltpu.CompilerParams(vmem_limit_bytes=4 * 1024 * 1024),
    )(err, scaled, first_moment, second_moment)
    return (err.reshape(1, D, COLS), first, second, direction)


def solution(mesh):
    return jax.shard_map(
        local,
        mesh=mesh,
        in_specs=(
            P("dp", None, "shard"),
            P("dp", None, "shard"),
            P("shard", None),
            P(("dp", "shard"), None),
            P(("dp", "shard"), None),
        ),
        out_specs=(
            P("dp", None, "shard"),
            P(("dp", "shard"), None),
            P(("dp", "shard"), None),
            P(("dp", "shard"), None),
        ),
        check_vma=False,
    )
```

time: 138 us -> 61.8 us (0.45)
  blocking collectives: 77.8 us -> 0 us
  Pallas kernels: 0 us -> 61 us
  other arithmetic: 15.6 us -> 0 us
  matrix products: 15.2 us -> 0 us
  waiting for transfers between devices: 15 us -> 0 us
  starting transfers between devices: 7.33 us -> 0 us
  local copies, waits for them, and re-layouts: 3.97 us -> 0.01 us
  between operations: 2.13 us -> 0.67 us
    all_to_all x3 -> x0, blocking collectives: 61.9 us -> none  [the longest x2 34.7 us: sent_to_all(): lax.all_to_all(jnp.broadcast_to(x[None], (count, *x.shape)), axis, 0, 0,...]
    pallas_call x0 -> x2, Pallas kernels: none -> 61 us  [the longest x1 58.9 us: local(): pl.pallas_call(kernel, out_shape=(jax.ShapeDtypeStruct(shape3, BF16), jax...]
    all_gather x1 -> x0, blocking collectives: 15.9 us -> none  [local(): left_raw = lax.all_gather(row_share, 'shard', axis=0, tiled=True)]
    all_to_all x1 -> x0, waiting for transfers between devices: 15 us -> none  [sent_to_all(): lax.all_to_all(jnp.broadcast_to(x[None], (count, *x.shape)), axis, 0, 0,...]
    dot_general x5 -> x0, matrix products: 13.5 us -> none  [the longest x1 7.79 us: local(): update = jnp.dot(left_orth, right_mean.T, precision=lax.Precision.HIGHEST)]
    all_to_all x1 -> x0, starting transfers between devices: 7.33 us -> none  [sent_to_all(): lax.all_to_all(jnp.broadcast_to(x[None], (count, *x.shape)), axis, 0, 0,...]
    another operation x5 -> x0, other arithmetic: 6.67 us -> none  [the longest x3 3.59 us: orthonormal(): jnp.linalg.cholesky(gram_matrix + ridge_shift * jnp.eye(width, dtype=jnp....]
    reduce_sum x4 -> x0, other arithmetic: 5.28 us -> none  [the longest x2 2.26 us: taken_together(): return sent_to_all(x, axis).sum(axis=0)]
  transfers between devices with their start and end apart: 1 -> 0, of which waited for: 1 -> 0; matrix products, arithmetic and copies ran while one was open for 6% -> 0% of each run, Pallas kernels for 0% -> 0%
where the time goes in v2:
time: 61.8 us; the launch traced here: 61.7 us
  Pallas kernels  61 us (99%)
  between operations  0.67 us (1%)
    pallas_call x1, Pallas kernels, local(): pl.pallas_call(kernel, out_shape=(jax.ShapeDtypeStruct(shape3, BF16), jax...  58.9 us
    pallas_call x1, Pallas kernels, local(): pl.pallas_call(step_kernel, out_shape=(jax.ShapeDtypeStruct(shape3, BF16)...  2.18 us

profile of v2, /device:TPU:1, one launch (start us, length us, event | category | flops | bytes accessed | tf_op | source)
XLA Modules:
  0.0 61.7 jit_solution(12774955946154042221)
XLA Ops:
  0.6 0.0 copy-start
  0.6 0.0 copy-start.1
  0.7 58.9 %shard_map.84 = (bf16[8,512,384]{2,1,0:T(8,128)(2,1)S(1)}, f32[16,6144]{1,0:T(8,128)S(1)}) custom-call(f32[32,384]{1,0:T(8,128)} %bitcast.6, bf16[8,512,384]{2,1,0:T(8,128)(2,1)} %bitcast.4, bf16[8,512,384]{2,1,0:T(8,128)(2,1)} %bitcast.5), custom_call_target="tpu_custom_call" | custom-call | tf_op jit(solution)/shard_map/pallas_call | solution.py:291
  59.5 0.0 copy-done
  59.5 0.0 copy-done.1
  59.5 2.2 %shard_map.85 = (bf16[8,512,384]{2,1,0:T(8,128)(2,1)}, f32[16,6144]{1,0:T(8,128)}, f32[16,6144]{1,0:T(8,128)}, f32[16,6144]{1,0:T(8,128)}) custom-call(bf16[8,512,384]{2,1,0:T(8,128)(2,1)S(1)} %get-tuple-element.10.err_ref, f32[16,6144]{1,0:T(8,128)S(1)} %get-tuple-element.11.scaled_ref, f32[16,6144]{1,0:T(8,128)S(1)} %copy-done, f32[16,6144]{1,0:T(8,128)S(1)} %copy-done.1), custom_call_target="tpu_custom_call" | custom-call | tf_op jit(solution)/shard_map/pallas_call | solution.py:335
Async XLA Ops:
  0.6 58.9 %copy-start = (f32[16,6144]{1,0:T(8,128)S(1)}, f32[16,6144]{1,0:T(8,128)}, u32[]{:S(2)}) copy-start(f32[16,6144]{1,0:T(8,128)} %first_ref.1) | copy-start | bytes 1179652
  0.6 58.9 %copy-start.1 = (f32[16,6144]{1,0:T(8,128)S(1)}, f32[16,6144]{1,0:T(8,128)}, u32[]{:S(2)}) copy-start(f32[16,6144]{1,0:T(8,128)} %second_ref.1) | copy-start | bytes 1179652

commit v3 on v2

--- a/solution.py
+++ b/solution.py
@@ -15,6 +15,8 @@
 ROWS = D // CHUNKS
 COLS = F // SH
 OWN = D // (DP * SH)
+PIECES = (R // 8) * (COLS // 128)
+AHEAD = 3
 
 CLIP_LEVEL = 0.9
 BETA_ONE = 0.9
@@ -67,10 +69,10 @@
     right_hbm, grad_hbm, errb_hbm,
     err_ref, scaled_ref,
     right_buf, grad_buf, errb_buf, merged, part, core_in, half, dp_in, z_in, left_raw,
-    left_split, left_stack, right_out, right_in, right_all, right_raw, blocks,
+    left_split, left_stack, right_out, right_in, right_all, planes, owned,
     load_g, load_e, load_m,
     s_core, r_core, s_dp, r_dp, s_z, r_z, s_dpa, r_dpa, s_ca, r_ca,
-    s_rr, r_rr, s_ra, r_ra, s_bz, r_bz, s_bc, r_bc,
+    s_rr, r_rr, s_ra, r_ra, s_bz, r_bz, s_pl, r_pl, s_bc, r_bc,
 ):
     i = lax.axis_index("dp")
     j = lax.axis_index("shard")
@@ -117,18 +119,24 @@
     pl.semaphore_signal(barrier, inc=1, device_id=(i, other), device_id_type=MESH)
     load_right = pltpu.make_async_copy(right_hbm, right_buf, load_m)
     load_right.start()
-    for k in range(CHUNKS):
+
+    def load(k):
         a = pltpu.make_async_copy(grad_hbm.at[k], grad_buf.at[k], load_g.at[k])
         b = pltpu.make_async_copy(errb_hbm.at[k], errb_buf.at[k], load_e.at[k])
         a.start()
         b.start()
         loads.append((a, b))
 
+    for k in range(AHEAD):
+        load(k)
+
     load_right.wait()
     right_low = right_buf[...].astype(BF16)
     for k in range(CHUNKS):
         for copy in loads[k]:
             copy.wait()
+        if k + AHEAD < CHUNKS:
+            load(k + AHEAD)
         total = (grad_buf[k].astype(F32) + errb_buf[k].astype(F32)).astype(BF16)
         merged[4 * k : 4 * (k + 1)] = total.reshape(4, 128, COLS)
         product = mm(right_low, total, NT)
@@ -191,79 +199,121 @@
         right_sum = right_sum + mm(stack, merged[pl.ds(first, 4)].reshape(ROWS, COLS), NN)
     right_part = right_sum[:R] + right_sum[R : 2 * R] + right_sum[2 * R :]
     for p in range(DP):
-        right_out[p] = right_part[2 * p : 2 * p + 2]
+        g, t = (p % PIECES) // 3, p % 3
+        right_out[p] = right_part[8 * g : 8 * (g + 1), 128 * t : 128 * (t + 1)]
     for d in dp_far:
         p = dp_peer(d)
         send(right_out.at[p], right_in.at[i], s_rr.at[d], r_rr.at[i], p, j)
     right_in[i] = right_out[i]
     inverse = split(triangular_inverse(fold(gram_sum, 3)))
     inverse = jnp.concatenate([jnp.concatenate([t] * 3, axis=1) for t in inverse], axis=0)
+
+    def orthonormal(stack):
+        wide = mm(inverse, stack, NN)
+        return wide[:R] + wide[R : 2 * R] + wide[2 * R :]
+
     for d in dp_near:
         p = dp_peer(d)
         remote(right_out.at[p], right_in.at[p], s_rr.at[d], r_rr.at[p], p, j).wait_recv()
     total = right_in[0]
     for p in range(1, DP):
         total = total + right_in[p]
-    right_all[i] = total * (1.0 / DP)
+    total = total * (1.0 / DP)
+    right_all[i] = total
+    planes[c, i, z] = total
+    for d in z_far:
+        send(planes.at[c, i, z], planes.at[c, i, z], s_bz.at[d], r_bz.at[z], i, 2 * z_peer(d) + c)
     for d in dp_far:
         send(right_all.at[i], right_all.at[i], s_ra.at[d], r_ra.at[i], dp_peer(d), j)
     ortho_sum = jnp.zeros((2 * R, 2 * R), F32)
     for k in range(CHUNKS):
-        wide = mm(inverse, left_split[k], NN)
-        high, mid, _ = split(wide[:R] + wide[R : 2 * R] + wide[2 * R :])
+        high, mid, _ = split(orthonormal(left_split[k]))
         stack = jnp.concatenate([high, mid], axis=0)
         ortho_sum = ortho_sum + mm(stack, stack, NT)
         left_stack[32 * k : 32 * (k + 1)] = jnp.concatenate([high, high, mid, mid], axis=0).T.reshape(32, OWN, 128)
     ortho_gram = fold(ortho_sum, 2)
+    for d in z_near:
+        p = z_peer(d)
+        remote(planes.at[c, i, p], planes.at[c, i, p], s_bz.at[d], r_bz.at[p], i, 2 * p + c).wait_recv()
+    def spread():
+        for d in dp_far:
+            yield remote(planes.at[c, i], planes.at[c, i], s_pl.at[d], r_pl.at[i], dp_peer(d), j)
+        yield remote(planes.at[c, i], planes.at[c, i], s_bc.at[i], r_bc.at[i], i, other)
+
+    @pl.when(i < PIECES)
+    def _():
+        for copy in spread():
+            copy.start()
+
     for d in dp_near:
         p = dp_peer(d)
         remote(right_all.at[p], right_all.at[p], s_ra.at[d], r_ra.at[p], p, j).wait_recv()
-    for p in range(DP):
-        right_raw[2 * p : 2 * p + 2] = right_all[p]
-    wide = mm(inverse, jnp.concatenate(split(right_raw[...]), axis=0), NN)
-    blocks[j] = wide[:R] + wide[R : 2 * R] + wide[2 * R :]
-    for d in z_far:
-        send(blocks.at[j], blocks.at[j], s_bz.at[d], r_bz.at[z], i, 2 * z_peer(d) + c)
-    send(blocks.at[j], blocks.at[j], s_bc.at[z], r_bc.at[z], i, other)
+
+    def stacked(pieces):
+        raw = jnp.concatenate(
+            [jnp.concatenate([pieces[3 * g + t] for t in range(3)], axis=1) for g in range(R // 8)], axis=0
+        )
+        high, mid, _ = split(orthonormal(jnp.concatenate(split(raw), axis=0)))
+        return jnp.concatenate([high, mid, high, mid], axis=0)
+
+    mine_stack = stacked([right_all[p] for p in range(PIECES)])
     own = left_stack[DP * i + j]
-
-    def stacked(block):
-        high, mid, _ = split(block)
-        return jnp.concatenate([high, mid, high, mid], axis=0)
-
-    mine_stack = stacked(blocks[j])
     for k in range(CHUNKS):
         rows = left_stack[32 * k : 32 * (k + 1)].reshape(ROWS, 128)
         whole = merged[4 * k : 4 * (k + 1)].reshape(ROWS, COLS)
         err_ref[k] = (whole.astype(F32) - mm(rows, mine_stack, NN)).astype(BF16)
-    for d in z_near:
-        p = z_peer(d)
-        q = 2 * p + c
-        remote(blocks.at[q], blocks.at[q], s_bz.at[d], r_bz.at[p], i, q).wait_recv()
-        send(blocks.at[q], blocks.at[q], s_bc.at[p], r_bc.at[p], i, other)
-    for p in range(ZN):
-        q = 2 * p + 1 - c
-        remote(blocks.at[q], blocks.at[q], s_bc.at[p], r_bc.at[p], i, other).wait_recv()
+
+    def relay(d):
+        p = dp_peer(d)
+        return p, remote(planes.at[c, p], planes.at[c, p], s_bc.at[p], r_bc.at[p], i, other)
+
+    for d in dp_near:
+        p, copy = relay(d)
+
+        @pl.when(p < PIECES)
+        def _():
+            remote(planes.at[c, p], planes.at[c, p], s_pl.at[d], r_pl.at[p], p, j).wait_recv()
+            copy.start()
+
     square = jnp.zeros((2 * R, 2 * R), F32)
-    rows = []
-    for q in range(SH):
-        stack = stacked(blocks[q])
-        square = square + mm(stack[: 2 * R], stack[: 2 * R], NT)
-        rows.append(mm(own, stack, NN))
+    for n in range(2):
+        core = c if n == 0 else 1 - c
+        if n == 1:
+            for p in range(PIECES):
+                remote(planes.at[core, p], planes.at[core, p], s_bc.at[p], r_bc.at[p], i, other).wait_recv()
+        for k in range(ZN):
+            stack = stacked([planes[core, p, k] for p in range(PIECES)])
+            square = square + mm(stack[: 2 * R], stack[: 2 * R], NT)
+            owned[2 * k + core] = mm(own, stack, NN)
     norm = jnp.sqrt(jnp.sum(fold(square, 2) * ortho_gram, keepdims=True))
     clip_level = CLIP_LEVEL * (float(R * (D + F)) ** 0.5)
     scale = clip_level / jnp.maximum(norm, clip_level)
     for q in range(SH):
-        scaled_ref[:, COLS * q : COLS * (q + 1)] = rows[q] * scale
+        scaled_ref[:, COLS * q : COLS * (q + 1)] = owned[q] * scale
     finish()
+    for d in dp_near:
+        p, copy = relay(d)
+
+        @pl.when(p < PIECES)
+        def _():
+            copy.wait_send()
+
+    @pl.when(i < PIECES)
+    def _():
+        for copy in spread():
+            copy.wait_send()
 
 
 def step_kernel(
     err_ref, scaled_ref, first_ref, second_ref, err_hbm, first_hbm, second_hbm, direction_hbm,
     first_res, second_res, direction_res, out_e, out_m,
 ):
-    outs = [pltpu.make_async_copy(err_ref, err_hbm, out_e)]
-    outs[0].start()
+    outs = []
+    for k in range(4):
+        chunks = pl.ds(k * CHUNKS // 4, CHUNKS // 4)
+        copy = pltpu.make_async_copy(err_ref.at[chunks], err_hbm.at[chunks], out_e.at[k])
+        copy.start()
+        outs.append(copy)
     pieces = 4
     width = F // pieces
     for q in range(pieces):
@@ -306,11 +356,11 @@
             vmem((2 * DP, R, 128), F32),
             vmem((CHUNKS, 3 * R, ROWS), BF16),
             vmem((DP * SH, OWN, 128), BF16),
-            vmem((DP, 2, COLS), F32),
-            vmem((DP, 2, COLS), F32),
-            vmem((DP, 2, COLS), F32),
-            vmem((R, COLS), F32),
-            vmem((SH, R, COLS), F32),
+            vmem((DP, 8, 128), F32),
+            vmem((DP, 8, 128), F32),
+            vmem((DP, 8, 128), F32),
+            vmem((2, DP, ZN, 8, 128), F32),
+            vmem((SH, OWN, COLS), F32),
             dma((CHUNKS,)), dma((CHUNKS,)), dma(()),
             dma((4,)), dma((4,)),
             dma((DP,)), dma((DP,)),
@@ -320,7 +370,8 @@
             dma((DP,)), dma((DP,)),
             dma((DP,)), dma((DP,)),
             dma((ZN,)), dma((ZN,)),
-            dma((ZN,)), dma((ZN,)),
+            dma((DP,)), dma((DP,)),
+            dma((DP,)), dma((DP,)),
         ],
         compiler_params=pltpu.CompilerParams(
             collective_id=0, has_side_effects=True, vmem_limit_bytes=28 * 1024 * 1024
@@ -339,7 +390,7 @@
         out_specs=(pl.BlockSpec(memory_space=pltpu.HBM),) * 4,
         scratch_shapes=[
             vmem((OWN, F), F32), vmem((OWN, F), F32), vmem((OWN, F), F32),
-            dma(()), dma((3, 4)),
+            dma((4,)), dma((3, 4)),
         ],
         compiler_params=pltpu.CompilerParams(vmem_limit_bytes=4 * 1024 * 1024),
     )(err, scaled, first_moment, second_moment)

time: 61.8 us -> 58.6 us (0.948)
  Pallas kernels: 61 us -> 57.8 us
    pallas_call x1, Pallas kernels: 58.9 us -> 55.6 us  [local(): pl.pallas_call(kernel, out_shape=(jax.ShapeDtypeStruct(shape3, BF16), jax...]
where the time goes in v3:
time: 58.6 us; the launch traced here: 58.4 us
  Pallas kernels  57.8 us (99%)
  between operations  0.67 us (1%)
    pallas_call x1, Pallas kernels, local(): pl.pallas_call(kernel, out_shape=(jax.ShapeDtypeStruct(shape3, BF16), jax...  55.6 us
    pallas_call x1, Pallas kernels, local(): pl.pallas_call(step_kernel, out_shape=(jax.ShapeDtypeStruct(shape3, BF16)...  2.2 us

profile of v3, /device:TPU:1, one launch (start us, length us, event | category | flops | bytes accessed | tf_op | source)
XLA Modules:
  0.0 58.4 jit_solution(13129113267889233673)
XLA Ops:
  0.6 0.0 copy-start
  0.6 0.0 copy-start.1
  0.7 55.6 %shard_map.84 = (bf16[8,512,384]{2,1,0:T(8,128)(2,1)S(1)}, f32[16,6144]{1,0:T(8,128)S(1)}) custom-call(f32[32,384]{1,0:T(8,128)} %bitcast.6, bf16[8,512,384]{2,1,0:T(8,128)(2,1)} %bitcast.4, bf16[8,512,384]{2,1,0:T(8,128)(2,1)} %bitcast.5), custom_call_target="tpu_custom_call" | custom-call | tf_op jit(solution)/shard_map/pallas_call | solution.py:341
  56.2 0.0 copy-done
  56.2 0.0 copy-done.1
  56.2 2.2 %shard_map.85 = (bf16[8,512,384]{2,1,0:T(8,128)(2,1)}, f32[16,6144]{1,0:T(8,128)}, f32[16,6144]{1,0:T(8,128)}, f32[16,6144]{1,0:T(8,128)}) custom-call(bf16[8,512,384]{2,1,0:T(8,128)(2,1)S(1)} %get-tuple-element.10.err_ref, f32[16,6144]{1,0:T(8,128)S(1)} %get-tuple-element.11.scaled_ref, f32[16,6144]{1,0:T(8,128)S(1)} %copy-done, f32[16,6144]{1,0:T(8,128)S(1)} %copy-done.1), custom_call_target="tpu_custom_call" | custom-call | tf_op jit(solution)/shard_map/pallas_call | solution.py:386
Async XLA Ops:
  0.6 55.6 %copy-start = (f32[16,6144]{1,0:T(8,128)S(1)}, f32[16,6144]{1,0:T(8,128)}, u32[]{:S(2)}) copy-start(f32[16,6144]{1,0:T(8,128)} %first_ref.1) | copy-start | bytes 1179652
  0.6 55.6 %copy-start.1 = (f32[16,6144]{1,0:T(8,128)S(1)}, f32[16,6144]{1,0:T(8,128)}, u32[]{:S(2)}) copy-start(f32[16,6144]{1,0:T(8,128)} %second_ref.1) | copy-start | bytes 1179652

commit v4 on v3

--- a/solution.py
+++ b/solution.py
@@ -17,6 +17,7 @@
 OWN = D // (DP * SH)
 PIECES = (R // 8) * (COLS // 128)
 AHEAD = 3
+PANEL = 8
 
 CLIP_LEVEL = 0.9
 BETA_ONE = 0.9
@@ -45,6 +46,10 @@
 def fold(full, n):
     rows = sum(full[R * a : R * (a + 1)] for a in range(n))
     return sum(rows[:, R * a : R * (a + 1)] for a in range(n))
+
+
+def fold_lanes(wide):
+    return wide[:, :R] + wide[:, R : 2 * R] + wide[:, 2 * R :]
 
 
 def triangular_inverse(gram_matrix):
@@ -56,11 +61,18 @@
     work = jnp.concatenate([shifted, jnp.where(eye, 1.0, 0.0)], axis=1)
     wide_row = lax.broadcasted_iota(jnp.int32, (R, 2 * R), 0)
     wide_col = lax.broadcasted_iota(jnp.int32, (R, 2 * R), 1)
-    for k in range(R - 1):
-        column = jnp.broadcast_to(work[:, k : k + 1], (R, 2 * R))
-        pivot = column[k : k + 1]
-        line = work[k : k + 1] * (1.0 / pivot)
-        work = work - jnp.where(wide_row > k, column, 0.0) * line
+    for k in range(0, R, PANEL):
+        columns = [jnp.broadcast_to(work[:, k + b : k + b + 1], (R, 2 * R)) for b in range(PANEL)]
+        rows = [work[k + b : k + b + 1] for b in range(PANEL)]
+        for b in range(PANEL):
+            inverse = 1.0 / columns[b][k + b : k + b + 1]
+            line = rows[b] * inverse
+            below = jnp.where(wide_row > k + b, columns[b], 0.0)
+            for a in range(b + 1, PANEL):
+                entry = columns[b][k + a : k + a + 1]
+                columns[a] = columns[a] - columns[b] * (entry * inverse)
+                rows[a] = rows[a] - entry * line
+            work = work - below * line
     diagonal = jnp.sum(jnp.where(wide_row == wide_col, work, 0.0), axis=1, keepdims=True)
     return work[:, R : 2 * R] * lax.rsqrt(diagonal)
 
@@ -69,10 +81,10 @@
     right_hbm, grad_hbm, errb_hbm,
     err_ref, scaled_ref,
     right_buf, grad_buf, errb_buf, merged, part, core_in, half, dp_in, z_in, left_raw,
-    left_split, left_stack, right_out, right_in, right_all, planes, owned,
+    left_split, left_stack, right_out, right_in, right_all, planes, norms,
     load_g, load_e, load_m,
     s_core, r_core, s_dp, r_dp, s_z, r_z, s_dpa, r_dpa, s_ca, r_ca,
-    s_rr, r_rr, s_ra, r_ra, s_bz, r_bz, s_pl, r_pl, s_bc, r_bc,
+    s_rr, r_rr, s_ra, r_ra, s_bz, r_bz, s_pl, r_pl, s_bc, r_bc, s_nz, r_nz, s_nc, r_nc,
 ):
     i = lax.axis_index("dp")
     j = lax.axis_index("shard")
@@ -177,26 +189,34 @@
     for d in dp_far:
         send(left_raw.at[mine], left_raw.at[mine], s_dpa.at[d], r_dpa.at[i], dp_peer(d), j)
     send(left_raw.at[mine], left_raw.at[mine], s_ca.at[i], r_ca.at[i], i, other)
-    for d in dp_near:
-        p = dp_peer(d)
-        q = DP * c + p
-        remote(left_raw.at[q], left_raw.at[q], s_dpa.at[d], r_dpa.at[p], p, j).wait_recv()
-        send(left_raw.at[q], left_raw.at[q], s_ca.at[p], r_ca.at[p], i, other)
-    gram_sum = jnp.zeros((3 * R, 3 * R), F32)
-    right_sum = jnp.zeros((3 * R, COLS), F32)
-    for k in range(CHUNKS):
-        if k < 4:
-            first = DP * c + 4 * k
-        else:
-            first = DP * (1 - c) + 4 * (k - 4)
-            for p in range(4 * (k - 4), 4 * (k - 3)):
-                q = DP * (1 - c) + p
-                remote(left_raw.at[q], left_raw.at[q], s_ca.at[p], r_ca.at[p], i, other).wait_recv()
-        wide = jnp.concatenate([left_raw[first + t] for t in range(4)], axis=1)
+
+    def accumulate(sums, tiles):
+        wide = jnp.concatenate([left_raw[q] for q in tiles], axis=1)
         stack = jnp.concatenate(split(wide), axis=0)
-        left_split[first // 4] = stack
-        gram_sum = gram_sum + mm(stack, stack, NT)
-        right_sum = right_sum + mm(stack, merged[pl.ds(first, 4)].reshape(ROWS, COLS), NN)
+        for n, q in enumerate(tiles):
+            left_split[q] = stack[:, 128 * n : 128 * (n + 1)]
+        rows = jnp.concatenate([merged[q] for q in tiles], axis=0)
+        return sums[0] + mm(stack, stack, NT), sums[1] + mm(stack, rows, NN)
+
+    sums = jnp.zeros((3 * R, 3 * R), F32), jnp.zeros((3 * R, COLS), F32)
+    order = [0] + dp_near
+    for g in range(4):
+        group = order[4 * g : 4 * (g + 1)]
+        for d in group:
+            p = dp_peer(d)
+            q = DP * c + p
+            if d:
+                remote(left_raw.at[q], left_raw.at[q], s_dpa.at[d], r_dpa.at[p], p, j).wait_recv()
+                send(left_raw.at[q], left_raw.at[q], s_ca.at[p], r_ca.at[p], i, other)
+        sums = accumulate(sums, [DP * c + dp_peer(d) for d in group])
+    for g in range(4):
+        group = order[4 * g : 4 * (g + 1)]
+        for d in group:
+            p = dp_peer(d)
+            q = DP * (1 - c) + p
+            remote(left_raw.at[q], left_raw.at[q], s_ca.at[p], r_ca.at[p], i, other).wait_recv()
+        sums = accumulate(sums, [DP * (1 - c) + dp_peer(d) for d in group])
+    gram_sum, right_sum = sums
     right_part = right_sum[:R] + right_sum[R : 2 * R] + right_sum[2 * R :]
     for p in range(DP):
         g, t = (p % PIECES) // 3, p % 3
@@ -205,8 +225,8 @@
         p = dp_peer(d)
         send(right_out.at[p], right_in.at[i], s_rr.at[d], r_rr.at[i], p, j)
     right_in[i] = right_out[i]
-    inverse = split(triangular_inverse(fold(gram_sum, 3)))
-    inverse = jnp.concatenate([jnp.concatenate([t] * 3, axis=1) for t in inverse], axis=0)
+    inverse_parts = split(triangular_inverse(fold(gram_sum, 3)))
+    inverse = jnp.concatenate([jnp.concatenate([t] * 3, axis=1) for t in inverse_parts], axis=0)
 
     def orthonormal(stack):
         wide = mm(inverse, stack, NN)
@@ -227,11 +247,24 @@
         send(right_all.at[i], right_all.at[i], s_ra.at[d], r_ra.at[i], dp_peer(d), j)
     ortho_sum = jnp.zeros((2 * R, 2 * R), F32)
     for k in range(CHUNKS):
-        high, mid, _ = split(orthonormal(left_split[k]))
+        wide = jnp.concatenate([left_split[4 * k + t] for t in range(4)], axis=1)
+        high, mid, _ = split(orthonormal(wide))
         stack = jnp.concatenate([high, mid], axis=0)
         ortho_sum = ortho_sum + mm(stack, stack, NT)
         left_stack[32 * k : 32 * (k + 1)] = jnp.concatenate([high, high, mid, mid], axis=0).T.reshape(32, OWN, 128)
     ortho_gram = fold(ortho_sum, 2)
+    pick = (
+        lax.broadcasted_iota(jnp.int32, (OWN, 128), 1)
+        == lax.broadcasted_iota(jnp.int32, (OWN, 128), 0) + OWN * (j % 8)
+    )
+    own = mm(jnp.where(pick, 1.0, 0.0).astype(BF16), left_split[2 * i + j // 8], NT).astype(BF16)
+    own = fold_lanes(mm(own, inverse, NT))
+    own = mm(
+        jnp.concatenate(split(own), axis=1),
+        jnp.concatenate([jnp.concatenate([t] * 3, axis=0) for t in inverse_parts], axis=1),
+        NN,
+    )
+    own = fold_lanes(own)
     for d in z_near:
         p = z_peer(d)
         remote(planes.at[c, i, p], planes.at[c, i, p], s_bz.at[d], r_bz.at[p], i, 2 * p + c).wait_recv()
@@ -249,20 +282,37 @@
         p = dp_peer(d)
         remote(right_all.at[p], right_all.at[p], s_ra.at[d], r_ra.at[p], p, j).wait_recv()
 
-    def stacked(pieces):
+    def raw_stack(pieces):
         raw = jnp.concatenate(
             [jnp.concatenate([pieces[3 * g + t] for t in range(3)], axis=1) for g in range(R // 8)], axis=0
         )
-        high, mid, _ = split(orthonormal(jnp.concatenate(split(raw), axis=0)))
-        return jnp.concatenate([high, mid, high, mid], axis=0)
-
-    mine_stack = stacked([right_all[p] for p in range(PIECES)])
-    own = left_stack[DP * i + j]
+        return jnp.concatenate(split(raw), axis=0)
+
+    high, mid, _ = split(orthonormal(raw_stack([right_all[p] for p in range(PIECES)])))
+    mine_stack = jnp.concatenate([high, mid, high, mid], axis=0)
+    square = fold(mm(mine_stack[: 2 * R], mine_stack[: 2 * R], NT), 2)
+    norms[c, z] = jnp.broadcast_to(jnp.sum(square * ortho_gram, keepdims=True), (8, 128))
+    for d in z_far:
+        send(norms.at[c, z], norms.at[c, z], s_nz.at[d], r_nz.at[z], i, 2 * z_peer(d) + c)
+    send(norms.at[c, z], norms.at[c, z], s_nc.at[z], r_nc.at[z], i, other)
     for k in range(CHUNKS):
         rows = left_stack[32 * k : 32 * (k + 1)].reshape(ROWS, 128)
         whole = merged[4 * k : 4 * (k + 1)].reshape(ROWS, COLS)
         err_ref[k] = (whole.astype(F32) - mm(rows, mine_stack, NN)).astype(BF16)
 
+    for d in z_near:
+        p = z_peer(d)
+        remote(norms.at[c, p], norms.at[c, p], s_nz.at[d], r_nz.at[p], i, 2 * p + c).wait_recv()
+        send(norms.at[c, p], norms.at[c, p], s_nc.at[p], r_nc.at[p], i, other)
+    for p in range(ZN):
+        remote(norms.at[1 - c, p], norms.at[1 - c, p], s_nc.at[p], r_nc.at[p], i, other).wait_recv()
+    total = norms[0, 0]
+    for k in range(1, SH):
+        total = total + norms[k // ZN, k % ZN]
+    clip_level = CLIP_LEVEL * (float(R * (D + F)) ** 0.5)
+    scale = clip_level / jnp.maximum(jnp.sqrt(total[0:1, 0:1]), clip_level)
+    own_stack = jnp.concatenate([jnp.concatenate([t] * 3, axis=1) for t in split(own * scale)], axis=0)
+
     def relay(d):
         p = dp_peer(d)
         return p, remote(planes.at[c, p], planes.at[c, p], s_bc.at[p], r_bc.at[p], i, other)
@@ -275,21 +325,14 @@
             remote(planes.at[c, p], planes.at[c, p], s_pl.at[d], r_pl.at[p], p, j).wait_recv()
             copy.start()
 
-    square = jnp.zeros((2 * R, 2 * R), F32)
     for n in range(2):
         core = c if n == 0 else 1 - c
         if n == 1:
             for p in range(PIECES):
                 remote(planes.at[core, p], planes.at[core, p], s_bc.at[p], r_bc.at[p], i, other).wait_recv()
         for k in range(ZN):
-            stack = stacked([planes[core, p, k] for p in range(PIECES)])
-            square = square + mm(stack[: 2 * R], stack[: 2 * R], NT)
-            owned[2 * k + core] = mm(own, stack, NN)
-    norm = jnp.sqrt(jnp.sum(fold(square, 2) * ortho_gram, keepdims=True))
-    clip_level = CLIP_LEVEL * (float(R * (D + F)) ** 0.5)
-    scale = clip_level / jnp.maximum(norm, clip_level)
-    for q in range(SH):
-        scaled_ref[:, COLS * q : COLS * (q + 1)] = owned[q] * scale
+            wide = mm(own_stack, raw_stack([planes[core, p, k] for p in range(PIECES)]), NN)
+            scaled_ref[2 * k + core] = wide[:OWN] + wide[OWN : 2 * OWN] + wide[2 * OWN :]
     finish()
     for d in dp_near:
         p, copy = relay(d)
@@ -314,20 +357,20 @@
         copy = pltpu.make_async_copy(err_ref.at[chunks], err_hbm.at[chunks], out_e.at[k])
         copy.start()
         outs.append(copy)
-    pieces = 4
-    width = F // pieces
-    for q in range(pieces):
-        lanes = pl.ds(width * q, width)
-        scaled = scaled_ref[:, lanes]
-        first = BETA_ONE * first_ref[:, lanes] + (1.0 - BETA_ONE) * scaled
-        second = BETA_TWO * second_ref[:, lanes] + (1.0 - BETA_TWO) * scaled * scaled
-        first_res[:, lanes] = first
-        second_res[:, lanes] = second
-        direction_res[:, lanes] = first / (jnp.sqrt(second) + EPSILON)
+    for g in range(4):
+        for q in range(4 * g, 4 * (g + 1)):
+            lanes = slice(COLS * q, COLS * (q + 1))
+            scaled = scaled_ref[q]
+            first = BETA_ONE * first_ref[:, lanes] + (1.0 - BETA_ONE) * scaled
+            second = BETA_TWO * second_ref[:, lanes] + (1.0 - BETA_TWO) * scaled * scaled
+            first_res[:, lanes] = first
+            second_res[:, lanes] = second
+            direction_res[:, lanes] = first / (jnp.sqrt(second) + EPSILON)
+        lanes = pl.ds(4 * COLS * g, 4 * COLS)
         for n, (res, hbm) in enumerate(
             ((first_res, first_hbm), (second_res, second_hbm), (direction_res, direction_hbm))
         ):
-            copy = pltpu.make_async_copy(res.at[:, lanes], hbm.at[:, lanes], out_m.at[n, q])
+            copy = pltpu.make_async_copy(res.at[:, lanes], hbm.at[:, lanes], out_m.at[n, g])
             copy.start()
             outs.append(copy)
     for copy in outs:
@@ -340,7 +383,7 @@
     vmem = pltpu.VMEM
     err, scaled = pl.pallas_call(
         kernel,
-        out_shape=(jax.ShapeDtypeStruct(shape3, BF16), jax.ShapeDtypeStruct((OWN, F), F32)),
+        out_shape=(jax.ShapeDtypeStruct(shape3, BF16), jax.ShapeDtypeStruct((SH, OWN, COLS), F32)),
         in_specs=[pl.BlockSpec(memory_space=pltpu.HBM)] * 3,
         out_specs=(pl.BlockSpec(memory_space=pltpu.VMEM),) * 2,
         scratch_shapes=[
@@ -354,13 +397,13 @@
             vmem((DP, R, 128), F32),
             vmem((ZN, R, 128), F32),
             vmem((2 * DP, R, 128), F32),
-            vmem((CHUNKS, 3 * R, ROWS), BF16),
+            vmem((2 * DP, 3 * R, 128), BF16),
             vmem((DP * SH, OWN, 128), BF16),
             vmem((DP, 8, 128), F32),
             vmem((DP, 8, 128), F32),
             vmem((DP, 8, 128), F32),
             vmem((2, DP, ZN, 8, 128), F32),
-            vmem((SH, OWN, COLS), F32),
+            vmem((2, ZN, 8, 128), F32),
             dma((CHUNKS,)), dma((CHUNKS,)), dma(()),
             dma((4,)), dma((4,)),
             dma((DP,)), dma((DP,)),
@@ -372,6 +415,8 @@
             dma((ZN,)), dma((ZN,)),
             dma((DP,)), dma((DP,)),
             dma((DP,)), dma((DP,)),
+            dma((ZN,)), dma((ZN,)),
+            dma((ZN,)), dma((ZN,)),
         ],
         compiler_params=pltpu.CompilerParams(
             collective_id=0, has_side_effects=True, vmem_limit_bytes=28 * 1024 * 1024

time: 58.6 us -> 55.4 us (0.945)
  Pallas kernels: 57.8 us -> 54.5 us
    pallas_call x1, Pallas kernels: 55.6 us -> 52.3 us  [local(): pl.pallas_call(kernel, out_shape=(jax.ShapeDtypeStruct(shape3, BF16), jax...]
where the time goes in v4:
time: 55.4 us; the launch traced here: 55.2 us
  Pallas kernels  54.5 us (98%)
  between operations  0.67 us (1%)
    pallas_call x1, Pallas kernels, local(): pl.pallas_call(kernel, out_shape=(jax.ShapeDtypeStruct(shape3, BF16), jax...  52.3 us
    pallas_call x1, Pallas kernels, local(): pl.pallas_call(step_kernel, out_shape=(jax.ShapeDtypeStruct(shape3, BF16)...  2.2 us

profile of v4, /device:TPU:1, one launch (start us, length us, event | category | flops | bytes accessed | tf_op | source)
XLA Modules:
  0.0 55.2 jit_solution(9418348019873886573)
XLA Ops:
  0.6 0.0 copy-start
  0.6 0.0 copy-start.1
  0.7 52.3 %shard_map.84 = (bf16[8,512,384]{2,1,0:T(8,128)(2,1)S(1)}, f32[16,16,384]{2,1,0:T(8,128)S(1)}) custom-call(f32[32,384]{1,0:T(8,128)} %bitcast.6, bf16[8,512,384]{2,1,0:T(8,128)(2,1)} %bitcast.4, bf16[8,512,384]{2,1,0:T(8,128)(2,1)} %bitcast.5), custom_call_target="tpu_custom_call" | custom-call | tf_op jit(solution)/shard_map/pallas_call | solution.py:384
  53.0 0.0 copy-done
  53.0 0.0 copy-done.1
  53.0 2.2 %shard_map.85 = (bf16[8,512,384]{2,1,0:T(8,128)(2,1)}, f32[16,6144]{1,0:T(8,128)}, f32[16,6144]{1,0:T(8,128)}, f32[16,6144]{1,0:T(8,128)}) custom-call(bf16[8,512,384]{2,1,0:T(8,128)(2,1)S(1)} %get-tuple-element.10.err_ref, f32[16,16,384]{2,1,0:T(8,128)S(1)} %get-tuple-element.11.scaled_ref, f32[16,6144]{1,0:T(8,128)S(1)} %copy-done, f32[16,6144]{1,0:T(8,128)S(1)} %copy-done.1), custom_call_target="tpu_custom_call" | custom-call | tf_op jit(solution)/shard_map/pallas_call | solution.py:431
Async XLA Ops:
  0.6 52.4 %copy-start = (f32[16,6144]{1,0:T(8,128)S(1)}, f32[16,6144]{1,0:T(8,128)}, u32[]{:S(2)}) copy-start(f32[16,6144]{1,0:T(8,128)} %first_ref.1) | copy-start | bytes 1179652
  0.6 52.4 %copy-start.1 = (f32[16,6144]{1,0:T(8,128)S(1)}, f32[16,6144]{1,0:T(8,128)}, u32[]{:S(2)}) copy-start(f32[16,6144]{1,0:T(8,128)} %second_ref.1) | copy-start | bytes 1179652

commit v5 on v4

--- a/solution.py
+++ b/solution.py
@@ -18,6 +18,8 @@
 PIECES = (R // 8) * (COLS // 128)
 AHEAD = 3
 PANEL = 8
+EARLY = 3
+HALF = 4
 
 CLIP_LEVEL = 0.9
 BETA_ONE = 0.9
@@ -52,16 +54,18 @@
     return wide[:, :R] + wide[:, R : 2 * R] + wide[:, 2 * R :]
 
 
-def triangular_inverse(gram_matrix):
+def shifted_pair(gram_matrix):
     row = lax.broadcasted_iota(jnp.int32, (R, R), 0)
     col = lax.broadcasted_iota(jnp.int32, (R, R), 1)
     eye = row == col
     trace = jnp.sum(jnp.where(eye, gram_matrix, 0.0), keepdims=True)
     shifted = gram_matrix + jnp.where(eye, 1e-06 * trace / R, 0.0)
-    work = jnp.concatenate([shifted, jnp.where(eye, 1.0, 0.0)], axis=1)
+    return jnp.concatenate([shifted, jnp.where(eye, 1.0, 0.0)], axis=1)
+
+
+def eliminate(work, panels):
     wide_row = lax.broadcasted_iota(jnp.int32, (R, 2 * R), 0)
-    wide_col = lax.broadcasted_iota(jnp.int32, (R, 2 * R), 1)
-    for k in range(0, R, PANEL):
+    for k in panels:
         columns = [jnp.broadcast_to(work[:, k + b : k + b + 1], (R, 2 * R)) for b in range(PANEL)]
         rows = [work[k + b : k + b + 1] for b in range(PANEL)]
         for b in range(PANEL):
@@ -73,13 +77,19 @@
                 columns[a] = columns[a] - columns[b] * (entry * inverse)
                 rows[a] = rows[a] - entry * line
             work = work - below * line
+    return work
+
+
+def triangular_inverse(work):
+    wide_row = lax.broadcasted_iota(jnp.int32, (R, 2 * R), 0)
+    wide_col = lax.broadcasted_iota(jnp.int32, (R, 2 * R), 1)
     diagonal = jnp.sum(jnp.where(wide_row == wide_col, work, 0.0), axis=1, keepdims=True)
     return work[:, R : 2 * R] * lax.rsqrt(diagonal)
 
 
 def kernel(
     right_hbm, grad_hbm, errb_hbm,
-    err_ref, scaled_ref,
+    err_ref, rows_ref, scale_ref,
     right_buf, grad_buf, errb_buf, merged, part, core_in, half, dp_in, z_in, left_raw,
     left_split, left_stack, right_out, right_in, right_all, planes, norms,
     load_g, load_e, load_m,
@@ -122,6 +132,7 @@
     def finish():
         for copy in sends:
             copy.wait_send()
+        sends.clear()
 
     barrier = pltpu.get_barrier_semaphore()
     for d in dp_far:
@@ -225,13 +236,8 @@
         p = dp_peer(d)
         send(right_out.at[p], right_in.at[i], s_rr.at[d], r_rr.at[i], p, j)
     right_in[i] = right_out[i]
-    inverse_parts = split(triangular_inverse(fold(gram_sum, 3)))
-    inverse = jnp.concatenate([jnp.concatenate([t] * 3, axis=1) for t in inverse_parts], axis=0)
-
-    def orthonormal(stack):
-        wide = mm(inverse, stack, NN)
-        return wide[:R] + wide[R : 2 * R] + wide[2 * R :]
-
+    panels = list(range(0, R, PANEL))
+    work = eliminate(shifted_pair(fold(gram_sum, 3)), panels[:EARLY])
     for d in dp_near:
         p = dp_peer(d)
         remote(right_out.at[p], right_in.at[p], s_rr.at[d], r_rr.at[p], p, j).wait_recv()
@@ -245,13 +251,37 @@
         send(planes.at[c, i, z], planes.at[c, i, z], s_bz.at[d], r_bz.at[z], i, 2 * z_peer(d) + c)
     for d in dp_far:
         send(right_all.at[i], right_all.at[i], s_ra.at[d], r_ra.at[i], dp_peer(d), j)
-    ortho_sum = jnp.zeros((2 * R, 2 * R), F32)
-    for k in range(CHUNKS):
-        wide = jnp.concatenate([left_split[4 * k + t] for t in range(4)], axis=1)
-        high, mid, _ = split(orthonormal(wide))
-        stack = jnp.concatenate([high, mid], axis=0)
-        ortho_sum = ortho_sum + mm(stack, stack, NT)
-        left_stack[32 * k : 32 * (k + 1)] = jnp.concatenate([high, high, mid, mid], axis=0).T.reshape(32, OWN, 128)
+    inverse_parts = split(triangular_inverse(eliminate(work, panels[EARLY:])))
+    inverse = jnp.concatenate([jnp.concatenate([t] * 3, axis=1) for t in inverse_parts], axis=0)
+
+    def orthonormal(stack):
+        wide = mm(inverse, stack, NN)
+        return wide[:R] + wide[R : 2 * R] + wide[2 * R :]
+
+    def left_rows(chunks, ortho_sum):
+        for k in chunks:
+            wide = jnp.concatenate([left_split[4 * k + t] for t in range(4)], axis=1)
+            high, mid, _ = split(orthonormal(wide))
+            stack = jnp.concatenate([high, mid], axis=0)
+            ortho_sum = ortho_sum + mm(stack, stack, NT)
+            left_stack[32 * k : 32 * (k + 1)] = jnp.concatenate([high, high, mid, mid], axis=0).T.reshape(32, OWN, 128)
+        return ortho_sum
+
+    ortho_sum = left_rows(range(HALF), jnp.zeros((2 * R, 2 * R), F32))
+    for d in z_near:
+        p = z_peer(d)
+        remote(planes.at[c, i, p], planes.at[c, i, p], s_bz.at[d], r_bz.at[p], i, 2 * p + c).wait_recv()
+    def spread():
+        for d in dp_far:
+            yield remote(planes.at[c, i], planes.at[c, i], s_pl.at[d], r_pl.at[i], dp_peer(d), j)
+        yield remote(planes.at[c, i], planes.at[c, i], s_bc.at[i], r_bc.at[i], i, other)
+
+    @pl.when(i < PIECES)
+    def _():
+        for copy in spread():
+            copy.start()
+
+    ortho_sum = left_rows(range(HALF, CHUNKS), ortho_sum)
     ortho_gram = fold(ortho_sum, 2)
     pick = (
         lax.broadcasted_iota(jnp.int32, (OWN, 128), 1)
@@ -265,19 +295,7 @@
         NN,
     )
     own = fold_lanes(own)
-    for d in z_near:
-        p = z_peer(d)
-        remote(planes.at[c, i, p], planes.at[c, i, p], s_bz.at[d], r_bz.at[p], i, 2 * p + c).wait_recv()
-    def spread():
-        for d in dp_far:
-            yield remote(planes.at[c, i], planes.at[c, i], s_pl.at[d], r_pl.at[i], dp_peer(d), j)
-        yield remote(planes.at[c, i], planes.at[c, i], s_bc.at[i], r_bc.at[i], i, other)
-
-    @pl.when(i < PIECES)
-    def _():
-        for copy in spread():
-            copy.start()
-
+    finish()
     for d in dp_near:
         p = dp_peer(d)
         remote(right_all.at[p], right_all.at[p], s_ra.at[d], r_ra.at[p], p, j).wait_recv()
@@ -300,31 +318,30 @@
         whole = merged[4 * k : 4 * (k + 1)].reshape(ROWS, COLS)
         err_ref[k] = (whole.astype(F32) - mm(rows, mine_stack, NN)).astype(BF16)
 
+    def relay(d):
+        p = dp_peer(d)
+        return p, remote(planes.at[c, p], planes.at[c, p], s_bc.at[p], r_bc.at[p], i, other)
+
+    for d in dp_near:
+        p, copy = relay(d)
+
+        @pl.when(p < PIECES)
+        def _():
+            remote(planes.at[c, p], planes.at[c, p], s_pl.at[d], r_pl.at[p], p, j).wait_recv()
+            copy.start()
+
+    finish()
+
+    @pl.when(i < PIECES)
+    def _():
+        for copy in spread():
+            copy.wait_send()
+
     for d in z_near:
         p = z_peer(d)
         remote(norms.at[c, p], norms.at[c, p], s_nz.at[d], r_nz.at[p], i, 2 * p + c).wait_recv()
         send(norms.at[c, p], norms.at[c, p], s_nc.at[p], r_nc.at[p], i, other)
-    for p in range(ZN):
-        remote(norms.at[1 - c, p], norms.at[1 - c, p], s_nc.at[p], r_nc.at[p], i, other).wait_recv()
-    total = norms[0, 0]
-    for k in range(1, SH):
-        total = total + norms[k // ZN, k % ZN]
-    clip_level = CLIP_LEVEL * (float(R * (D + F)) ** 0.5)
-    scale = clip_level / jnp.maximum(jnp.sqrt(total[0:1, 0:1]), clip_level)
-    own_stack = jnp.concatenate([jnp.concatenate([t] * 3, axis=1) for t in split(own * scale)], axis=0)
-
-    def relay(d):
-        p = dp_peer(d)
-        return p, remote(planes.at[c, p], planes.at[c, p], s_bc.at[p], r_bc.at[p], i, other)
-
-    for d in dp_near:
-        p, copy = relay(d)
-
-        @pl.when(p < PIECES)
-        def _():
-            remote(planes.at[c, p], planes.at[c, p], s_pl.at[d], r_pl.at[p], p, j).wait_recv()
-            copy.start()
-
+    own_stack = jnp.concatenate([jnp.concatenate([t] * 3, axis=1) for t in split(own)], axis=0)
     for n in range(2):
         core = c if n == 0 else 1 - c
         if n == 1:
@@ -332,7 +349,14 @@
                 remote(planes.at[core, p], planes.at[core, p], s_bc.at[p], r_bc.at[p], i, other).wait_recv()
         for k in range(ZN):
             wide = mm(own_stack, raw_stack([planes[core, p, k] for p in range(PIECES)]), NN)
-            scaled_ref[2 * k + core] = wide[:OWN] + wide[OWN : 2 * OWN] + wide[2 * OWN :]
+            rows_ref[2 * k + core] = wide[:OWN] + wide[OWN : 2 * OWN] + wide[2 * OWN :]
+    for p in range(ZN):
+        remote(norms.at[1 - c, p], norms.at[1 - c, p], s_nc.at[p], r_nc.at[p], i, other).wait_recv()
+    total = norms[0, 0]
+    for k in range(1, SH):
+        total = total + norms[k // ZN, k % ZN]
+    clip_level = CLIP_LEVEL * (float(R * (D + F)) ** 0.5)
+    scale_ref[...] = clip_level / jnp.maximum(jnp.sqrt(total), clip_level)
     finish()
     for d in dp_near:
         p, copy = relay(d)
@@ -341,14 +365,9 @@
         def _():
             copy.wait_send()
 
-    @pl.when(i < PIECES)
-    def _():
-        for copy in spread():
-            copy.wait_send()
-
 
 def step_kernel(
-    err_ref, scaled_ref, first_ref, second_ref, err_hbm, first_hbm, second_hbm, direction_hbm,
+    err_ref, rows_ref, scale_ref, first_ref, second_ref, err_hbm, first_hbm, second_hbm, direction_hbm,
     first_res, second_res, direction_res, out_e, out_m,
 ):
     outs = []
@@ -357,10 +376,11 @@
         copy = pltpu.make_async_copy(err_ref.at[chunks], err_hbm.at[chunks], out_e.at[k])
         copy.start()
         outs.append(copy)
+    scale = scale_ref[0:1, 0:1]
     for g in range(4):
         for q in range(4 * g, 4 * (g + 1)):
             lanes = slice(COLS * q, COLS * (q + 1))
-            scaled = scaled_ref[q]
+            scaled = rows_ref[q] * scale
             first = BETA_ONE * first_ref[:, lanes] + (1.0 - BETA_ONE) * scaled
             second = BETA_TWO * second_ref[:, lanes] + (1.0 - BETA_TWO) * scaled * scaled
             first_res[:, lanes] = first
@@ -381,11 +401,11 @@
     shape3 = (CHUNKS, ROWS, COLS)
     dma = pltpu.SemaphoreType.DMA
     vmem = pltpu.VMEM
-    err, scaled = pl.pallas_call(
+    err, rows, scale = pl.pallas_call(
         kernel,
-        out_shape=(jax.ShapeDtypeStruct(shape3, BF16), jax.ShapeDtypeStruct((SH, OWN, COLS), F32)),
+        out_shape=(jax.ShapeDtypeStruct(shape3, BF16), jax.ShapeDtypeStruct((SH, OWN, COLS), F32), jax.ShapeDtypeStruct((8, 128), F32)),
         in_specs=[pl.BlockSpec(memory_space=pltpu.HBM)] * 3,
-        out_specs=(pl.BlockSpec(memory_space=pltpu.VMEM),) * 2,
+        out_specs=(pl.BlockSpec(memory_space=pltpu.VMEM),) * 3,
         scratch_shapes=[
             vmem((R, COLS), F32),
             vmem(shape3, BF16),
@@ -431,14 +451,14 @@
     err, first, second, direction = pl.pallas_call(
         step_kernel,
         out_shape=(jax.ShapeDtypeStruct(shape3, BF16), own, own, own),
-        in_specs=[pl.BlockSpec(memory_space=pl.ANY)] + [pl.BlockSpec(memory_space=pltpu.VMEM)] * 3,
+        in_specs=[pl.BlockSpec(memory_space=pl.ANY)] + [pl.BlockSpec(memory_space=pltpu.VMEM)] * 4,
         out_specs=(pl.BlockSpec(memory_space=pltpu.HBM),) * 4,
         scratch_shapes=[
             vmem((OWN, F), F32), vmem((OWN, F), F32), vmem((OWN, F), F32),
             dma((4,)), dma((3, 4)),
         ],
         compiler_params=pltpu.CompilerParams(vmem_limit_bytes=4 * 1024 * 1024),
-    )(err, scaled, first_moment, second_moment)
+    )(err, rows, scale, first_moment, second_moment)
     return (err.reshape(1, D, COLS), first, second, direction)
 
 

time: 55.4 us -> 54.8 us (0.989)
  Pallas kernels: 54.5 us -> 53.9 us
    pallas_call x1, Pallas kernels: 52.3 us -> 51.7 us  [local(): pl.pallas_call(kernel, out_shape=(jax.ShapeDtypeStruct(shape3, BF16), jax...]
where the time goes in v5:
time: 54.8 us; the launch traced here: 54.6 us
  Pallas kernels  53.9 us (98%)
  between operations  0.67 us (1%)
    pallas_call x1, Pallas kernels, local(): pl.pallas_call(kernel, out_shape=(jax.ShapeDtypeStruct(shape3, BF16), jax...  51.7 us
    pallas_call x1, Pallas kernels, local(): pl.pallas_call(step_kernel, out_shape=(jax.ShapeDtypeStruct(shape3, BF16)...  2.23 us

profile of v5, /device:TPU:1, one launch (start us, length us, event | category | flops | bytes accessed | tf_op | source)
XLA Modules:
  0.0 54.6 jit_solution(6624221528879250194)
XLA Ops:
  0.6 0.0 copy-start
  0.6 0.0 copy-start.1
  0.7 51.7 %shard_map.84 = (bf16[8,512,384]{2,1,0:T(8,128)(2,1)S(1)}, f32[16,16,384]{2,1,0:T(8,128)S(1)}, f32[8,128]{1,0:T(8,128)S(1)}) custom-call(f32[32,384]{1,0:T(8,128)} %bitcast.6, bf16[8,512,384]{2,1,0:T(8,128)(2,1)} %bitcast.4, bf16[8,512,384]{2,1,0:T(8,128)(2,1)} %bitcast.5), custom_call_target="tpu_custom_call" | custom-call | tf_op jit(solution)/shard_map/pallas_call | solution.py:404
  52.4 0.0 copy-done
  52.4 0.0 copy-done.1
  52.4 2.2 %shard_map.85 = (bf16[8,512,384]{2,1,0:T(8,128)(2,1)}, f32[16,6144]{1,0:T(8,128)}, f32[16,6144]{1,0:T(8,128)}, f32[16,6144]{1,0:T(8,128)}) custom-call(bf16[8,512,384]{2,1,0:T(8,128)(2,1)S(1)} %get-tuple-element.11.err_ref, f32[16,16,384]{2,1,0:T(8,128)S(1)} %get-tuple-element.12.rows_ref, f32[8,128]{1,0:T(8,128)S(1)} %get-tuple-element.13.scale_ref, ...), custom_call_target="tpu_custom_call" | custom-call | tf_op jit(solution)/shard_map/pallas_call | solution.py:451
Async XLA Ops:
  0.6 51.7 %copy-start = (f32[16,6144]{1,0:T(8,128)S(1)}, f32[16,6144]{1,0:T(8,128)}, u32[]{:S(2)}) copy-start(f32[16,6144]{1,0:T(8,128)} %first_ref.1) | copy-start | bytes 1179652
  0.6 51.7 %copy-start.1 = (f32[16,6144]{1,0:T(8,128)S(1)}, f32[16,6144]{1,0:T(8,128)}, u32[]{:S(2)}) copy-start(f32[16,6144]{1,0:T(8,128)} %second_ref.1) | copy-start | bytes 1179652

commit v6 on v5

--- a/solution.py
+++ b/solution.py
@@ -167,17 +167,26 @@
             part[4 * k + t] = product[:, 128 * t : 128 * (t + 1)]
 
     pl.semaphore_wait(barrier, DP - 1 + ZN - 1 + 1)
+    x_order = (2, 1, 3, 0)
+
+    def piece(k):
+        return 4 * ((x + x_order[k]) % 4)
+
     for k in range(4):
-        send(part.at[pl.ds(DP * (1 - c) + 4 * k, 4)], core_in.at[pl.ds(4 * k, 4)], s_core.at[k], r_core.at[k], i, other)
+        q = piece(k)
+        send(part.at[pl.ds(DP * (1 - c) + q, 4)], core_in.at[pl.ds(q, 4)], s_core.at[k], r_core.at[k], i, other)
     for k in range(4):
+        q = piece(k)
         remote(
-            part.at[pl.ds(DP * c + 4 * k, 4)], core_in.at[pl.ds(4 * k, 4)], s_core.at[k], r_core.at[k], i, other
+            part.at[pl.ds(DP * c + q, 4)], core_in.at[pl.ds(q, 4)], s_core.at[k], r_core.at[k], i, other
         ).wait_recv()
-        for t in range(4 * k, 4 * k + 4):
-            half[t] = part[DP * c + t] + core_in[t]
-    for d in dp_far:
-        p = dp_peer(d)
-        send(half.at[p], dp_in.at[i], s_dp.at[d], r_dp.at[i], p, j)
+        for t in range(4):
+            half[q + t] = part[DP * c + q + t] + core_in[q + t]
+        for dy in (2, 1, 3, 0):
+            d = 4 * x_order[k] + dy
+            if d:
+                p = dp_peer(d)
+                send(half.at[p], dp_in.at[i], s_dp.at[d], r_dp.at[i], p, j)
     dp_in[i] = half[i]
     for d in dp_near:
         p = dp_peer(d)

time: 54.8 us -> 54.6 us (level)
  no operation moved by 1% of the time
where the time goes in v6:
time: 54.6 us; the launch traced here: 54.5 us
  Pallas kernels  53.8 us (99%)
  between operations  0.67 us (1%)
    pallas_call x1, Pallas kernels, local(): pl.pallas_call(kernel, out_shape=(jax.ShapeDtypeStruct(shape3, BF16), jax...  51.6 us
    pallas_call x1, Pallas kernels, local(): pl.pallas_call(step_kernel, out_shape=(jax.ShapeDtypeStruct(shape3, BF16)...  2.23 us

profile of v6, /device:TPU:1, one launch (start us, length us, event | category | flops | bytes accessed | tf_op | source)
XLA Modules:
  0.0 54.5 jit_solution(5178671968048941398)
XLA Ops:
  0.6 0.0 copy-start
  0.6 0.0 copy-start.1
  0.7 51.6 %shard_map.84 = (bf16[8,512,384]{2,1,0:T(8,128)(2,1)S(1)}, f32[16,16,384]{2,1,0:T(8,128)S(1)}, f32[8,128]{1,0:T(8,128)S(1)}) custom-call(f32[32,384]{1,0:T(8,128)} %bitcast.6, bf16[8,512,384]{2,1,0:T(8,128)(2,1)} %bitcast.4, bf16[8,512,384]{2,1,0:T(8,128)(2,1)} %bitcast.5), custom_call_target="tpu_custom_call" | custom-call | tf_op jit(solution)/shard_map/pallas_call | solution.py:413
  52.2 0.0 copy-done
  52.2 0.0 copy-done.1
  52.2 2.2 %shard_map.85 = (bf16[8,512,384]{2,1,0:T(8,128)(2,1)}, f32[16,6144]{1,0:T(8,128)}, f32[16,6144]{1,0:T(8,128)}, f32[16,6144]{1,0:T(8,128)}) custom-call(bf16[8,512,384]{2,1,0:T(8,128)(2,1)S(1)} %get-tuple-element.11.err_ref, f32[16,16,384]{2,1,0:T(8,128)S(1)} %get-tuple-element.12.rows_ref, f32[8,128]{1,0:T(8,128)S(1)} %get-tuple-element.13.scale_ref, ...), custom_call_target="tpu_custom_call" | custom-call | tf_op jit(solution)/shard_map/pallas_call | solution.py:460
Async XLA Ops:
  0.6 51.6 %copy-start = (f32[16,6144]{1,0:T(8,128)S(1)}, f32[16,6144]{1,0:T(8,128)}, u32[]{:S(2)}) copy-start(f32[16,6144]{1,0:T(8,128)} %first_ref.1) | copy-start | bytes 1179652
  0.6 51.6 %copy-start.1 = (f32[16,6144]{1,0:T(8,128)S(1)}, f32[16,6144]{1,0:T(8,128)}, u32[]{:S(2)}) copy-start(f32[16,6144]{1,0:T(8,128)} %second_ref.1) | copy-start | bytes 1179652
